TPU v7x, 256 devices: a whole 4x4x8 slice. The times are simulated.
256 devices in a mesh: leaf: 64 (over z, x, y_lo), panel: 4 (over y_hi, core).
Axes of the slice: x: 4, y: 4 (y_hi: 2, y_lo: 2; y = y_hi * 2 + y_lo), z: 8, core: 2. Of those that a mesh axis runs over, the one named last changes fastest.
Arguments:
- pix_cycle: bfloat16 [65536, 1536], P('leaf', 'panel'), may hold values from -6 to 6
- cycle_to_dissection: int32 [65536], replicated, may hold values from 0 to 65535, as said below
- subtree_of: int32 [64], replicated, may hold values from 0 to 63, each once
- fill_blocks: int32 [512, 12], replicated, may hold values 0 or 1
- leaf_shift: float32 [64, 1536], replicated, may hold values from 0.5 to 4
- separator_shift: float32 [1024], P('panel'), may hold values from 0.5 to 4
Outputs:
- leaf_factor: float32 [32768, 512], P('leaf', 'panel')
- leaf_coupling: float32 [65536, 512], P('leaf', 'panel')
- separator_factor: float32 [1024, 1024], P('leaf', 'panel')
Inputs may be any that keep to these rules, and one draw needn't show every extreme that they name: `cycle_to_dissection`: for every subtree t, positions t * 1024 to (t + 1) * 1024 - 1 name each cycle index of the form q * 1024 + t * 16 + o, with 0 <= o < 16 and 0 <= q < 64, exactly once.
All inputs are finite; a program needn't handle non-finite values.
Results may differ from a plain program's by a relative error of at most 0.0003.
Values may be sent and summed in bfloat16 or wider, within the bound.
A program may use at most 128 MiB of HBM per device.

v0:
```python
import jax
import jax.numpy as jnp
from jax import lax
from jax.sharding import PartitionSpec as P

KSUP = 512
SSEP = 1024
BLK = 128


def partner(array, axis, distance):
    return lax.ppermute(array, axis, [(i, i ^ 1 << distance) for i in range(lax.axis_size(axis))])


def per_device(
    pix_cycle, cycle_to_dissection, subtree_of, fill_blocks, leaf_shift, separator_shift
):
    leaves = lax.axis_size("leaf")
    panels = lax.axis_size("panel")
    rows_local, cols_local = pix_cycle.shape
    block_rows = rows_local // leaves
    leaf_index = lax.axis_index("leaf")
    panel_index = lax.axis_index("panel")
    subtree = subtree_of[leaf_index]
    outgoing = jnp.take(pix_cycle.reshape(leaves, block_rows, cols_local), subtree_of, axis=0)
    received = lax.all_to_all(
        outgoing.reshape(rows_local, cols_local), "leaf", split_axis=0, concat_axis=0, tiled=True
    )
    cycle_index = lax.dynamic_slice_in_dim(cycle_to_dissection, subtree * rows_local, rows_local)
    source = cycle_index // rows_local
    offset = cycle_index % rows_local - subtree * block_rows
    ordered = jnp.take(received, source * block_rows + offset, axis=0)
    design = lax.all_gather(ordered, "panel", axis=1, tiled=True)
    width = design.shape[1]
    col_blocks = width // BLK
    row_blocks = rows_local // BLK
    pattern = lax.dynamic_slice_in_dim(fill_blocks, subtree * row_blocks, row_blocks).astype(
        jnp.bfloat16
    )
    masked = (design.reshape(row_blocks, BLK, col_blocks, BLK) * pattern[:, None, :, None]).reshape(
        rows_local, width
    )
    front = (
        lax.dot_general(
            masked, masked, (((0,), (0,)), ((), ())), preferred_element_type=jnp.float32
        )
        / rows_local
    )
    front = front + jnp.diag(leaf_shift[subtree])
    lower = jnp.linalg.cholesky(front[:KSUP, :KSUP])
    coupling = lax.linalg.triangular_solve(
        lower, front[KSUP:, :KSUP], left_side=False, lower=True, transpose_a=True
    )
    own_width = KSUP // panels
    sep_width = SSEP // panels
    factor_cols = lax.dynamic_slice_in_dim(lower, panel_index * own_width, own_width, 1)
    coupling_cols = lax.dynamic_slice_in_dim(coupling, panel_index * own_width, own_width, 1)
    trailing = lax.dynamic_slice_in_dim(front[KSUP:, KSUP:], panel_index * sep_width, sep_width, 1)
    coupling_rows = lax.dynamic_slice_in_dim(coupling, panel_index * sep_width, sep_width, 0)
    update = trailing - jnp.dot(coupling, coupling_rows.T, precision=lax.Precision.HIGHEST)
    merged = update
    for bit_number in range(leaves.bit_length() - 1):
        merged = merged + partner(merged, "leaf", bit_number)
    row_ids = jnp.arange(SSEP, dtype=jnp.int32)[:, None]
    col_ids = panel_index * sep_width + jnp.arange(sep_width, dtype=jnp.int32)[None, :]
    diagonal = jnp.where(row_ids == col_ids, separator_shift[None, :], 0.0)
    separator = merged / leaves + diagonal
    whole = lax.all_gather(separator, "panel", axis=1, tiled=True)
    result = lax.dynamic_slice_in_dim(
        jnp.linalg.cholesky(whole), panel_index * sep_width, sep_width, 1
    )
    leaf_rows = SSEP // leaves
    result_rows = lax.dynamic_slice_in_dim(result, leaf_index * leaf_rows, leaf_rows, 0)
    return (factor_cols, coupling_cols, result_rows)


def solution(mesh):
    placed = (P("leaf", "panel"), P(), P(), P(), P(), P("panel"))
    return jax.shard_map(
        per_device,
        mesh=mesh,
        in_specs=placed,
        out_specs=(P("leaf", "panel"), P("leaf", "panel"), P("leaf", "panel")),
        check_vma=False,
    )
```

profile of v0, /device:TPU:1, one launch (start us, length us, event | category | flops | bytes accessed | tf_op | source)
XLA Modules:
  0.0 709.0 jit_solution(11335736581057258151)
XLA Ops:
  10.4 13.5 %all-to-all-start = ((bf16[64,16,384]{2,1,0:T(8,128)(2,1)}), bf16[64,16,384]{2,1,0:T(8,128)(2,1)S(1)}, u32[]{:S(2)}, u32[]{:S(2)}) async-start(bf16[64,16,384]{2,1,0:T(8,128)(2,1)} %broadcast_select_fusion), calls=%async_computation | async-start | bytes 1572864 | tf_op jit(solution)/shard_map/all_to_all | solution.py:26
  26.5 18.7 %all-to-all-done = bf16[64,16,384]{2,1,0:T(8,128)(2,1)S(1)} async-done(((bf16[64,16,384]{2,1,0:T(8,128)(2,1)}), bf16[64,16,384]{2,1,0:T(8,128)(2,1)S(1)}, u32[]{:S(2)}, u32[]{:S(2)}) %all-to-all-start) | async-done | bytes 786464 | tf_op jit(solution)/shard_map/all_to_all | solution.py:26
  45.2 3.9 gather_fusion.1
  53.5 2.5 copy.57
  56.0 4.7 copy.27
  62.2 22.5 %all-gather.3.cloned.1.call-done = bf16[1024,1536]{1,0:T(8,128)(2,1)} async-done(((bf16[1024,384]{1,0:T(8,128)(2,1)}), bf16[1024,1536]{1,0:T(8,128)(2,1)}) %all-gather.3.cloned.1.call-update) | async-done | bytes 3145744 | tf_op jit(solution)/shard_map/all_gather | solution.py:33
  84.7 10.6 %select_add_fusion = f32[1536,1536]{0,1:T(8,128)S(1)} fusion(f32[1536]{0:T(1024)S(1)} %dynamic-slice_reduce_fusion, bf16[1024,1536]{1,0:T(8,128)(2,1)} %all-gather.3.cloned.1.call-done, bf16[1024,1536]{1,0:T(8,128)(2,1)} %copy.27), kind=kOutput, calls=%fused_computation.5 | convolution fusion | flops 4842848256 | bytes 15734784 | tf_op jit(solution)/shard_map/dot_general | solution.py:44
  95.4 3.5 copy-done.3
  99.0 2.5 slice.261
  101.8 1.4 fusion.20
  103.3 11.7 %cholesky.280 = f32[128,128]{1,0:T(8,128)S(1)} custom-call(f32[128,128]{1,0:T(8,128)S(1)} %copy.30), custom_call_target="Cholesky" | custom-call | tf_op jit(solution)/shard_map/jit(cholesky)/cholesky | solution.py:50
  115.1 9.8 %custom-call.76 = f32[1,128,128]{1,2,0:T(8,128)S(1)} custom-call(f32[1,128,128]{2,1,0:T(8,128)S(1)} %get-tuple-element.65), custom_call_target="InvertDiagBlocksLowerTriangular" | custom-call | tf_op jit(solution)/shard_map/jit(cholesky)/cholesky/custom-call.1 | solution.py:50
  126.0 11.7 %cholesky.294 = f32[128,128]{1,0:T(8,128)S(1)} custom-call(f32[128,128]{1,0:T(8,128)S(1)} %copy.33), custom_call_target="Cholesky" | custom-call | tf_op jit(solution)/shard_map/jit(cholesky)/cholesky | solution.py:50
  137.8 10.2 %custom-call.77 = f32[1,128,128]{1,2,0:T(8,128)S(1)} custom-call(f32[1,128,128]{2,1,0:T(8,128)S(1)} %get-tuple-element.62), custom_call_target="InvertDiagBlocksLowerTriangular" | custom-call | tf_op jit(solution)/shard_map/jit(cholesky)/cholesky/custom-call.0 | solution.py:50
  148.9 11.7 %cholesky.315 = f32[128,128]{1,0:T(8,128)S(1)} custom-call(f32[128,128]{1,0:T(8,128)S(1)} %copy.36), custom_call_target="Cholesky" | custom-call | tf_op jit(solution)/shard_map/jit(cholesky)/cholesky | solution.py:50
  161.3 9.8 %custom-call.78 = f32[1,128,128]{1,2,0:T(8,128)S(1)} custom-call(f32[1,128,128]{2,1,0:T(8,128)S(1)} %get-tuple-element.59), custom_call_target="InvertDiagBlocksLowerTriangular" | custom-call | tf_op jit(solution)/shard_map/jit(cholesky)/cholesky/custom-call.2 | solution.py:50
  171.9 11.9 %cholesky.330 = f32[128,128]{1,0:T(8,128)S(1)} custom-call(f32[128,128]{1,0:T(8,128)S(1)} %copy.39), custom_call_target="Cholesky" | custom-call | tf_op jit(solution)/shard_map/jit(cholesky)/cholesky | solution.py:50
  188.8 8.0 %while.1 = (s32[]{:T(128)}, f32[512,512]{1,0:T(8,128)S(1)}, s32[4,2]{0,1:T(2,128)S(1)}, f32[4,128,128]{2,1,0:T(8,128)S(1)}, s32[]{:T(128)}) while((s32[]{:T(128)}, f32[512,512]{1,0:T(8,128)S(1)}, s32[4,2]{0,1:T(2,128)S(1)}, f32[4,128,128]{2,1,0:T(8,128)S(1)}, s32[]{:T(128)}) %tuple.53), condition=%wide.while_cond, body=%wide.while_body.sunk | while | flops 2 | bytes 131189 | solution.py:51
  191.4 1.4 bitcast_dynamic-update-slice_fusion.2
  196.8 39.3 %custom-call.68 = f32[4,128,128]{1,2,0:T(8,128)S(1)} custom-call(f32[4,128,128]{2,1,0:T(8,128)S(1)} %get-tuple-element.13), custom_call_target="InvertDiagBlocksLowerTriangular" | custom-call | tf_op jit(solution)/shard_map/triangular_solve | solution.py:51
  236.2 1.7 fusion.26
  237.8 1.7 convolution_subtract_fusion.2
  240.1 1.8 convolution_subtract_fusion.1
  242.5 2.2 fusion.8
  245.5 3.3 convolution_subtract_fusion
  249.2 24.2 %collective-permute-done = f32[1024,256]{0,1:T(8,128)S(1)} collective-permute-done((f32[1024,256]{0,1:T(8,128)S(1)}, f32[1024,256]{0,1:T(8,128)S(1)}, u32[]{:S(2)}, u32[]{:S(2)}) %collective-permute-start) | collective-permute-done | bytes 1048608 | tf_op jit(solution)/shard_map/ppermute | solution.py:12
  274.8 22.4 %collective-permute-done.1 = f32[1024,256]{0,1:T(8,128)S(1)} collective-permute-done((f32[1024,256]{0,1:T(8,128)S(1)}, f32[1024,256]{0,1:T(8,128)S(1)}, u32[]{:S(2)}, u32[]{:S(2)}) %collective-permute-start.1) | collective-permute-done | bytes 1048608 | tf_op jit(solution)/shard_map/ppermute | solution.py:12
  297.4 2.8 collective-permute-start.2
  300.1 21.6 %collective-permute-done.2 = f32[1024,256]{0,1:T(8,128)S(1)} collective-permute-done((f32[1024,256]{0,1:T(8,128)S(1)}, f32[1024,256]{0,1:T(8,128)S(1)}, u32[]{:S(2)}, u32[]{:S(2)}) %collective-permute-start.2) | collective-permute-done | bytes 1048608 | tf_op jit(solution)/shard_map/ppermute | solution.py:12
  323.2 20.6 %collective-permute-done.3 = f32[1024,256]{0,1:T(8,128)S(1)} collective-permute-done((f32[1024,256]{0,1:T(8,128)S(1)}, f32[1024,256]{0,1:T(8,128)S(1)}, u32[]{:S(2)}, u32[]{:S(2)}) %collective-permute-start.3) | collective-permute-done | bytes 1048608 | tf_op jit(solution)/shard_map/ppermute | solution.py:12
  344.1 2.4 collective-permute-start.4
  346.4 44.8 %collective-permute-done.4 = f32[1024,256]{0,1:T(8,128)S(1)} collective-permute-done((f32[1024,256]{0,1:T(8,128)S(1)}, f32[1024,256]{0,1:T(8,128)S(1)}, u32[]{:S(2)}, u32[]{:S(2)}) %collective-permute-start.4) | collective-permute-done | bytes 1048608 | tf_op jit(solution)/shard_map/ppermute | solution.py:12
  391.4 6.8 collective-permute-start.5
  398.2 45.6 %collective-permute-done.5 = f32[1024,256]{0,1:T(8,128)S(1)} collective-permute-done((f32[1024,256]{0,1:T(8,128)S(1)}, f32[1024,256]{0,1:T(8,128)S(1)}, u32[]{:S(2)}, u32[]{:S(2)}) %collective-permute-start.5) | collective-permute-done | bytes 1048608 | tf_op jit(solution)/shard_map/ppermute | solution.py:12
  446.0 1.7 constant_dynamic-slice_fusion.2
  447.7 37.1 %all-gather.5.cloned.1.call-done = f32[1024,1024]{0,1:T(8,128)} async-done(((f32[1024,256]{0,1:T(8,128)}), f32[1024,1024]{0,1:T(8,128)}) %all-gather.5.cloned.1.call-update) | async-done | bytes 4194320 | tf_op jit(solution)/shard_map/all_gather | solution.py:68
  484.8 5.7 copy.41
  490.5 4.4 fusion
  494.9 1.9 copy-done.2
  496.9 11.7 %cholesky.590 = f32[128,128]{1,0:T(8,128)S(1)} custom-call(f32[128,128]{1,0:T(8,128)S(1)} %cholesky.742), custom_call_target="Cholesky" | custom-call | tf_op jit(solution)/shard_map/jit(cholesky)/cholesky | solution.py:70
  508.6 2.5 cholesky.615
  511.8 9.8 %custom-call.69 = f32[1,128,128]{1,2,0:T(8,128)S(1)} custom-call(f32[1,128,128]{2,1,0:T(8,128)S(1)} %get-tuple-element.55), custom_call_target="InvertDiagBlocksLowerTriangular" | custom-call | tf_op jit(solution)/shard_map/jit(cholesky)/cholesky | solution.py:70
  521.6 2.4 constant_dynamic-update-slice_fusion
  523.9 1.5 convolution_subtract_fusion.3
  525.5 11.9 %cholesky.608 = f32[128,128]{1,0:T(8,128)S(1)} custom-call(f32[128,128]{1,0:T(8,128)S(1)} %cholesky.746), custom_call_target="Cholesky" | custom-call | tf_op jit(solution)/shard_map/jit(cholesky)/cholesky | solution.py:70
  538.6 9.8 %custom-call.70 = f32[1,128,128]{1,2,0:T(8,128)S(1)} custom-call(f32[1,128,128]{2,1,0:T(8,128)S(1)} %get-tuple-element.52), custom_call_target="InvertDiagBlocksLowerTriangular" | custom-call | tf_op jit(solution)/shard_map/jit(cholesky)/cholesky | solution.py:70
  549.7 2.1 convolution_subtract_fusion.4
  551.8 11.7 %cholesky.629 = f32[128,128]{1,0:T(8,128)S(1)} custom-call(f32[128,128]{1,0:T(8,128)S(1)} %cholesky.751), custom_call_target="Cholesky" | custom-call | tf_op jit(solution)/shard_map/jit(cholesky)/cholesky | solution.py:70
  564.8 9.8 %custom-call.71 = f32[1,128,128]{1,2,0:T(8,128)S(1)} custom-call(f32[1,128,128]{2,1,0:T(8,128)S(1)} %get-tuple-element.49), custom_call_target="InvertDiagBlocksLowerTriangular" | custom-call | tf_op jit(solution)/shard_map/jit(cholesky)/cholesky | solution.py:70
  575.8 2.3 convolution_subtract_fusion.5
  578.1 11.9 %cholesky.648 = f32[128,128]{1,0:T(8,128)S(1)} custom-call(f32[128,128]{1,0:T(8,128)S(1)} %cholesky.756), custom_call_target="Cholesky" | custom-call | tf_op jit(solution)/shard_map/jit(cholesky)/cholesky | solution.py:70
  591.3 9.8 %custom-call.72 = f32[1,128,128]{1,2,0:T(8,128)S(1)} custom-call(f32[1,128,128]{2,1,0:T(8,128)S(1)} %get-tuple-element.46), custom_call_target="InvertDiagBlocksLowerTriangular" | custom-call | tf_op jit(solution)/shard_map/jit(cholesky)/cholesky | solution.py:70
  602.2 2.3 convolution_subtract_fusion.6
  604.6 11.7 %cholesky.667 = f32[128,128]{1,0:T(8,128)S(1)} custom-call(f32[128,128]{1,0:T(8,128)S(1)} %cholesky.761), custom_call_target="Cholesky" | custom-call | tf_op jit(solution)/shard_map/jit(cholesky)/cholesky | solution.py:70
  617.6 10.2 %custom-call.79 = f32[1,128,128]{1,2,0:T(8,128)S(1)} custom-call(f32[1,128,128]{2,1,0:T(8,128)S(1)} %get-tuple-element.43), custom_call_target="InvertDiagBlocksLowerTriangular" | custom-call | tf_op jit(solution)/shard_map/jit(cholesky)/cholesky/custom-call.1 | solution.py:70
  628.8 2.3 convolution_subtract_fusion.8
  631.1 11.7 %cholesky.683 = f32[128,128]{1,0:T(8,128)S(1)} custom-call(f32[128,128]{1,0:T(8,128)S(1)} %cholesky.766), custom_call_target="Cholesky" | custom-call | tf_op jit(solution)/shard_map/jit(cholesky)/cholesky | solution.py:70
  644.1 9.8 %custom-call.80 = f32[1,128,128]{1,2,0:T(8,128)S(1)} custom-call(f32[1,128,128]{2,1,0:T(8,128)S(1)} %get-tuple-element.40), custom_call_target="InvertDiagBlocksLowerTriangular" | custom-call | tf_op jit(solution)/shard_map/jit(cholesky)/cholesky/custom-call.0 | solution.py:70
  654.8 2.0 convolution_subtract_fusion.10
  656.9 11.8 %cholesky.699 = f32[128,128]{1,0:T(8,128)S(1)} custom-call(f32[128,128]{1,0:T(8,128)S(1)} %cholesky.771), custom_call_target="Cholesky" | custom-call | tf_op jit(solution)/shard_map/jit(cholesky)/cholesky | solution.py:70
  670.1 9.8 %custom-call.81 = f32[1,128,128]{1,2,0:T(8,128)S(1)} custom-call(f32[1,128,128]{2,1,0:T(8,128)S(1)} %get-tuple-element.37), custom_call_target="InvertDiagBlocksLowerTriangular" | custom-call | tf_op jit(solution)/shard_map/jit(cholesky)/cholesky/custom-call.2 | solution.py:70
  680.7 1.8 convolution_subtract_fusion.11
  682.5 11.7 %cholesky.713 = f32[128,128]{1,0:T(8,128)S(1)} custom-call(f32[128,128]{1,0:T(8,128)S(1)} %convolution_subtract_fusion.11), custom_call_target="Cholesky" | custom-call | tf_op jit(solution)/shard_map/jit(cholesky)/cholesky | solution.py:70
  700.5 1.5 fusion.75
  (109 shorter events, 45.1 us)
Async XLA Ops:
  7.2 1.4 copy-start
  7.2 16.7 %copy-start.5 = (s32[64]{0:T(128)S(1)}, s32[64]{0:T(128)}, u32[]{:S(2)}) copy-start(s32[64]{0:T(128)} %param.14) | copy-start | bytes 772
  10.4 34.8 %all-to-all-start = ((bf16[64,16,384]{2,1,0:T(8,128)(2,1)}), bf16[64,16,384]{2,1,0:T(8,128)(2,1)S(1)}, u32[]{:S(2)}, u32[]{:S(2)}) async-start(bf16[64,16,384]{2,1,0:T(8,128)(2,1)} %broadcast_select_fusion), calls=%async_computation | async-start | bytes 1572864 | tf_op jit(solution)/shard_map/all_to_all | solution.py:26
  23.9 60.8 %all-gather.3.cloned.1.call-start = ((), (), s32[]{:S(2)}) async-start(), calls=%async_computation.1 | async-start | bytes 3932160 | tf_op jit(solution)/shard_map/all_gather | solution.py:33
  50.2 434.5 %all-gather.5.cloned.1.call-start = ((), (), s32[]{:S(2)}) async-start(), calls=%async_computation.2 | async-start | bytes 5242880 | tf_op jit(solution)/shard_map/all_gather | solution.py:68
  95.3 3.6 copy-start.3
  248.8 24.6 %collective-permute-start = (f32[1024,256]{0,1:T(8,128)S(1)}, f32[1024,256]{0,1:T(8,128)S(1)}, u32[]{:S(2)}, u32[]{:S(2)}) collective-permute-start(f32[1024,256]{0,1:T(8,128)S(1)} %convolution_subtract_fusion), channel_id=1, source_target_pairs={{0,4},{4,0},{8,12},{12,8},{16,20},{20,16},{24,28},{28,24},{32,36},... | collective-permute-start | bytes 3145736 | tf_op jit(solution)/shard_map/ppermute | solution.py:12
  273.5 23.7 %collective-permute-start.1 = (f32[1024,256]{0,1:T(8,128)S(1)}, f32[1024,256]{0,1:T(8,128)S(1)}, u32[]{:S(2)}, u32[]{:S(2)}) collective-permute-start(f32[1024,256]{0,1:T(8,128)S(1)} %add.191), channel_id=1, source_target_pairs={{0,8},{4,12},{8,0},{12,4},{16,24},{20,28},{24,16},{28,20},{32,40},... | collective-permute-start | bytes 3145736 | tf_op jit(solution)/shard_map/ppermute | solution.py:12
  297.4 146.4 %copy-start.4 = (f32[256]{0:T(256)S(1)}, f32[256]{0:T(256)}, u32[]{:S(2)}) copy-start(f32[256]{0:T(256)} %param.17) | copy-start | bytes 3076
  297.4 24.4 %collective-permute-start.2 = (f32[1024,256]{0,1:T(8,128)S(1)}, f32[1024,256]{0,1:T(8,128)S(1)}, u32[]{:S(2)}, u32[]{:S(2)}) collective-permute-start(f32[1024,256]{0,1:T(8,128)S(1)} %add.192), channel_id=1, source_target_pairs={{0,16},{4,20},{8,24},{12,28},{16,0},{20,4},{24,8},{28,12},{32,48},... | collective-permute-start | bytes 3145736 | tf_op jit(solution)/shard_map/ppermute | solution.py:12
  321.9 22.0 %collective-permute-start.3 = (f32[1024,256]{0,1:T(8,128)S(1)}, f32[1024,256]{0,1:T(8,128)S(1)}, u32[]{:S(2)}, u32[]{:S(2)}) collective-permute-start(f32[1024,256]{0,1:T(8,128)S(1)} %add.193), channel_id=1, source_target_pairs={{0,32},{4,36},{8,40},{12,44},{16,48},{20,52},{24,56},{28,60},{32,0... | collective-permute-start | bytes 3145736 | tf_op jit(solution)/shard_map/ppermute | solution.py:12
  344.1 47.2 %collective-permute-start.4 = (f32[1024,256]{0,1:T(8,128)S(1)}, f32[1024,256]{0,1:T(8,128)S(1)}, u32[]{:S(2)}, u32[]{:S(2)}) collective-permute-start(f32[1024,256]{0,1:T(8,128)S(1)} %add.194), channel_id=1, source_target_pairs={{0,64},{4,68},{8,72},{12,76},{16,80},{20,84},{24,88},{28,92},{32,9... | collective-permute-start | bytes 3145736 | tf_op jit(solution)/shard_map/ppermute | solution.py:12
  391.4 52.3 %collective-permute-start.5 = (f32[1024,256]{0,1:T(8,128)S(1)}, f32[1024,256]{0,1:T(8,128)S(1)}, u32[]{:S(2)}, u32[]{:S(2)}) collective-permute-start(f32[1024,256]{0,1:T(8,128)S(1)} %add.195), channel_id=1, source_target_pairs={{0,128},{4,132},{8,136},{12,140},{16,144},{20,148},{24,152},{28,15... | collective-permute-start | bytes 3145736 | tf_op jit(solution)/shard_map/ppermute | solution.py:12
  494.9 1.9 copy-start.2
  590.0 112.0 %copy-start.1 = (bf16[1024,384]{1,0:T(8,128)(2,1)S(1)}, bf16[1024,384]{1,0:T(8,128)(2,1)}, u32[]{:S(2)}) copy-start(bf16[1024,384]{1,0:T(8,128)(2,1)} %param.12) | copy-start | bytes 2359300
Sparse Core Ops, SparseCore 0:
  50.3 34.2 all-gather.2
  445.1 39.6 all-gather.4
where the time goes:
time: 716 us; the launch traced here: 709 us
  other arithmetic  307 us (43%)
  waiting for transfers between devices  257 us (36%)
  matrix products  48.5 us (7%)
  local copies, waits for them, and re-layouts  41.5 us (6%)
  starting transfers between devices  28.5 us (4%)
  between operations  26.2 us (4%)
    ppermute x6, waiting for transfers between devices, partner(): lax.ppermute(array, axis, [(i, i ^ 1 << distance) for i in range(lax.axis...  179 us
    another operation x31, other arithmetic, per_device(): jnp.linalg.cholesky(whole)  173 us
    another operation x14, other arithmetic, per_device(): lower = jnp.linalg.cholesky(front[:KSUP, :KSUP])  78.9 us
    another operation x4, other arithmetic, per_device(): lax.linalg.triangular_solve(lower, front[KSUP:, :KSUP], left_side=False,...  40.7 us
    all_gather x1, waiting for transfers between devices, per_device(): whole = lax.all_gather(separator, 'panel', axis=1, tiled=True)  37.1 us
    another operation x14, matrix products, per_device(): jnp.linalg.cholesky(whole)  23.1 us
    all_gather x1, waiting for transfers between devices, per_device(): design = lax.all_gather(ordered, 'panel', axis=1, tiled=True)  22.5 us
    all_to_all x1, waiting for transfers between devices, per_device(): lax.all_to_all(outgoing.reshape(rows_local, cols_local), 'leaf', split_ax...  18.7 us
  transfers between devices with their start and end apart: 9, of which 9 were waited for; matrix products, arithmetic and copies ran while one was open for 2% of the time, Pallas kernels for 0%

commit v1 on v0

v1 whole, which is shorter than its diff:
```python
import jax
import jax.numpy as jnp
from jax import lax
from jax.experimental import pallas as pl
from jax.experimental.pallas import tpu as pltpu
from jax.sharding import PartitionSpec as P

KSUP = 512
SSEP = 1024
FRONT = KSUP + SSEP
BLK = 128
SLAB = 16
HIGHEST = lax.Precision.HIGHEST
VMEM_LIMIT = 60 << 20


def row_of(values, index):
    return jnp.broadcast_to(values[index : index + 1, :], (8, BLK))


def twice(values):
    return jnp.concatenate([values, values], 0)


def factor_block(block):
    lanes8 = lax.broadcasted_iota(jnp.int32, (8, BLK), 1)
    lanes = lax.broadcasted_iota(jnp.int32, (SLAB, BLK), 1)
    subs = lax.broadcasted_iota(jnp.int32, (SLAB, BLK), 0)
    count = BLK // SLAB
    work = [block[SLAB * s : SLAB * (s + 1), :] for s in range(count)]
    scaled = [None] * count
    corner = [None] * count
    for s in range(count):
        base = SLAB * s
        own = work[s]
        inside = (lanes >= base) & (lanes < base + SLAB)
        cols = []
        for j in range(SLAB):
            first = 8 if j >= 8 else 0
            cols.append(jnp.broadcast_to(own[first:, base + j : base + j + 1], (SLAB - first, BLK)))
        below = {
            b: [
                jnp.broadcast_to(work[b][:, base + j : base + j + 1], (SLAB, BLK))
                for j in range(SLAB)
            ]
            for b in range(s + 1, count)
        }
        start = jnp.where(inside, jnp.where(lanes - base == subs, 1.0, 0.0), own)
        rows = [row_of(start, j) for j in range(SLAB)]
        inv_pivot, scale, mult = [], [], {}
        for k in range(SLAB):
            off = 8 if k >= 8 else 0
            pivot = row_of(cols[k], k - off)
            inverse = 1.0 / pivot
            inv_pivot.append(inverse)
            scale.append(lax.rsqrt(pivot))
            for j in range(k + 1, SLAB):
                mult[k, j] = row_of(cols[k], j - off) * inverse
            for j in range(k + 1, SLAB):
                if j >= 8:
                    source = cols[k] if k >= 8 else cols[k][8:, :]
                    cols[j] = cols[j] - source * mult[k, j]
                else:
                    cols[j] = cols[j] - cols[k] * twice(mult[k, j])
                rows[j] = rows[j] - mult[k, j] * rows[k]
        solved = [rows[k] * inv_pivot[k] for k in range(SLAB)]
        for i in reversed(range(SLAB)):
            for k in range(i):
                solved[k] = solved[k] - mult[k, i] * solved[i]
        for b in range(s + 1, count):
            rest = jnp.where(inside, 0.0, work[b])
            for k in range(SLAB):
                rest = rest - below[b][k] * twice(solved[k])
            work[b] = rest
        out = jnp.zeros((SLAB, BLK), jnp.float32)
        low = jnp.zeros((SLAB, BLK), jnp.float32)
        for k in range(SLAB):
            out = jnp.where(subs == k, twice(rows[k] * scale[k]), out)
            if k >= 8:
                column = jnp.concatenate(
                    [jnp.zeros((8, BLK), jnp.float32), cols[k] * scale[k]], 0
                )
            else:
                column = cols[k] * twice(scale[k])
            low = jnp.where((lanes == base + k) & (subs >= k), column, low)
        scaled[s] = out
        corner[s] = low
    full = jnp.concatenate(scaled, 0)
    corners = jnp.concatenate(corner, 0)
    row_ids = lax.broadcasted_iota(jnp.int32, (BLK, BLK), 0)
    col_ids = lax.broadcasted_iota(jnp.int32, (BLK, BLK), 1)
    factor = jnp.where(row_ids // SLAB > col_ids // SLAB, full.T, corners)
    inverse = jnp.where(row_ids >= col_ids, full, 0.0)
    return factor, inverse


def dot_nt(a, b, precision=HIGHEST):
    return lax.dot_general(
        a, b, (((1,), (1,)), ((), ())), precision=precision, preferred_element_type=jnp.float32
    )


def dot_tn(a, b):
    return lax.dot_general(a, b, (((0,), (0,)), ((), ())), preferred_element_type=jnp.float32)


def eliminate(matrix, panel_ref, at, strips):
    rows = matrix.shape[0]
    factor, inverse = factor_block(matrix[pl.ds(at, BLK), pl.ds(at, BLK)])
    panel = dot_nt(matrix[:, pl.ds(at, BLK)], inverse)
    row_ids = lax.broadcasted_iota(jnp.int32, (rows, BLK), 0)
    panel = jnp.where(row_ids >= at + BLK, panel, 0.0)
    panel_ref[...] = panel
    matrix[:, pl.ds(at, BLK)] = panel
    matrix[pl.ds(at, BLK), pl.ds(at, BLK)] = factor
    for top, bottom, width in strips:

        @pl.when(width > at + BLK)
        def _():
            matrix[top:bottom, :width] = matrix[top:bottom, :width] - dot_nt(
                panel_ref[top:bottom, :], panel_ref[:width, :]
            )


def leaf_kernel(
    spot, design, position, pattern, shift, factor_out, coupling_out, blocks_out,
    masked, front, panel_ref, trail,
):
    panel_index = spot[0]
    rows = design.shape[1]
    piece = design.shape[2]
    here = lax.broadcasted_iota(jnp.int32, (rows, rows), 0)
    chosen = jnp.where(here == position[0:1, :], 1.0, 0.0).astype(jnp.bfloat16)
    fill = jnp.concatenate(
        [jnp.broadcast_to(pattern[b : b + 1, :], (BLK, BLK)) for b in range(rows // BLK)], 0
    )
    touch = jnp.dot(chosen, fill.astype(jnp.bfloat16), preferred_element_type=jnp.float32)
    for c in range(FRONT // BLK):
        p, at = c * BLK // piece, c * BLK % piece
        keep = jnp.broadcast_to(touch[:, c : c + 1], (rows, BLK)).astype(jnp.bfloat16)
        masked[:, c * BLK : (c + 1) * BLK] = design[p, :, at : at + BLK] * keep
    scale = 1.0 / rows
    for top in range(0, FRONT, 512):
        front[top : top + 512, :] = dot_tn(masked[:, top : top + 512], masked[:, :KSUP]) * scale
    row_ids = lax.broadcasted_iota(jnp.int32, (BLK, BLK), 0)
    col_ids = lax.broadcasted_iota(jnp.int32, (BLK, BLK), 1)
    same = row_ids == col_ids
    for b in range(KSUP // BLK):
        span = slice(b * BLK, (b + 1) * BLK)
        front[span, span] = front[span, span] + jnp.where(same, shift[0:1, span], 0.0)
    last = SSEP // BLK - 1
    halves = (panel_index, last - panel_index)
    for h, block_row in enumerate(halves):
        at = pl.multiple_of(KSUP + block_row * BLK, BLK)
        trail[h * BLK : (h + 1) * BLK, :] = (
            dot_tn(masked[:, pl.ds(at, BLK)], masked[:, KSUP:]) * scale
        )
        corner = pl.ds(pl.multiple_of(block_row * BLK, BLK), BLK)
        span = slice(h * BLK, (h + 1) * BLK)
        trail[span, corner] = trail[span, corner] + jnp.where(same, shift[0:1, pl.ds(at, BLK)], 0.0)

    strips = [(0, 256, 256), (256, FRONT, KSUP)]

    def step(j, carry):
        at = pl.multiple_of(j * BLK, BLK)
        eliminate(front, panel_ref, at, strips)

        @pl.when(j == panel_index)
        def _():
            factor_out[...] = front[:KSUP, pl.ds(at, BLK)]
            coupling_out[...] = front[KSUP:, pl.ds(at, BLK)]

        return carry

    lax.fori_loop(0, KSUP // BLK, step, 0)
    for h, block_row in enumerate(halves):
        at = pl.multiple_of(KSUP + block_row * BLK, BLK)
        span = slice(h * BLK, (h + 1) * BLK)
        trail[span, :] = trail[span, :] - dot_nt(front[pl.ds(at, BLK), :], front[KSUP:, :])

    def pack(i, carry):
        second = i > panel_index
        top = pl.multiple_of(jnp.where(second, BLK, 0), BLK)
        left = pl.multiple_of(jnp.where(second, i - panel_index - 1, i) * BLK, BLK)
        blocks_out[pl.ds(pl.multiple_of(i * BLK, BLK), BLK), :] = trail[
            pl.ds(top, BLK), pl.ds(left, BLK)
        ]
        return carry

    lax.fori_loop(0, last + 2, pack, 0)


def separator_kernel(spot, blocks, shift, out, matrix, panel_ref):
    size = SSEP // BLK
    share = 1.0 / 64
    row_ids = lax.broadcasted_iota(jnp.int32, (BLK, BLK), 0)
    col_ids = lax.broadcasted_iota(jnp.int32, (BLK, BLK), 1)
    for r in range(size):
        for c in range(size):
            span = (slice(r * BLK, (r + 1) * BLK), slice(c * BLK, (c + 1) * BLK))
            if c > r:
                matrix[span] = jnp.zeros((BLK, BLK), jnp.float32)
                continue
            p = min(r, size - 1 - r)
            i = c if r == p else p + 1 + c
            value = blocks[p, i * BLK : (i + 1) * BLK, :] * share
            if c == r:
                value = value + jnp.where(row_ids == col_ids, shift[0:1, span[1]], 0.0)
            matrix[span] = value
    strips = [(t, t + 256, t + 256) for t in range(0, SSEP, 256)]

    def step(j, carry):
        eliminate(matrix, panel_ref, pl.multiple_of(j * BLK, BLK), strips)
        return carry

    lax.fori_loop(0, size, step, 0)
    top = pl.multiple_of(spot[0] * out.shape[0], out.shape[0])
    left = pl.multiple_of(spot[1] * out.shape[1], out.shape[1])
    out[...] = matrix[pl.ds(top, out.shape[0]), pl.ds(left, out.shape[1])]


VM = pl.BlockSpec(memory_space=pltpu.VMEM)
SM = pl.BlockSpec(memory_space=pltpu.SMEM)


def per_device(
    pix_cycle, cycle_to_dissection, subtree_of, fill_blocks, leaf_shift, separator_shift
):
    leaves = lax.axis_size("leaf")
    panels = lax.axis_size("panel")
    rows, piece = pix_cycle.shape
    block_rows = rows // leaves
    leaf_index = lax.axis_index("leaf")
    panel_index = lax.axis_index("panel")
    subtree = subtree_of[leaf_index]
    outgoing = jnp.take(pix_cycle.reshape(leaves, block_rows, piece), subtree_of, axis=0)
    received = lax.all_to_all(
        outgoing.reshape(rows, piece), "leaf", split_axis=0, concat_axis=0, tiled=True
    )
    design = lax.all_gather(received, "panel", axis=0)
    cycle_index = lax.dynamic_slice_in_dim(cycle_to_dissection, subtree * rows, rows)
    position = (cycle_index // rows) * block_rows + cycle_index % rows - subtree * block_rows
    row_blocks = rows // BLK
    pattern = lax.dynamic_slice_in_dim(fill_blocks, subtree * row_blocks, row_blocks)
    pattern = jnp.pad(pattern, ((0, 0), (0, BLK - pattern.shape[1]))).astype(jnp.float32)
    shift = lax.dynamic_slice_in_dim(leaf_shift, subtree, 1, 0)
    count = SSEP // BLK + 1
    factor_cols, coupling_cols, blocks = pl.pallas_call(
        leaf_kernel,
        out_shape=(
            jax.ShapeDtypeStruct((KSUP, KSUP // panels), jnp.float32),
            jax.ShapeDtypeStruct((SSEP, KSUP // panels), jnp.float32),
            jax.ShapeDtypeStruct((count * BLK, BLK), jnp.float32),
        ),
        in_specs=[SM, VM, VM, VM, VM],
        out_specs=(VM, VM, VM),
        scratch_shapes=[
            pltpu.VMEM((rows, FRONT), jnp.bfloat16),
            pltpu.VMEM((FRONT, KSUP), jnp.float32),
            pltpu.VMEM((FRONT, BLK), jnp.float32),
            pltpu.VMEM((2 * BLK, SSEP), jnp.float32),
        ],
        compiler_params=pltpu.CompilerParams(vmem_limit_bytes=VMEM_LIMIT),
        name="leaf_front",
    )(panel_index[None], design, position[None], pattern, shift)
    summed = lax.psum(blocks, "leaf")
    whole = lax.all_gather(summed, "panel", axis=0)
    shifts = lax.all_gather(separator_shift, "panel", axis=0, tiled=True)
    result_rows = pl.pallas_call(
        separator_kernel,
        out_shape=jax.ShapeDtypeStruct((SSEP // leaves, SSEP // panels), jnp.float32),
        in_specs=[SM, VM, VM],
        out_specs=VM,
        scratch_shapes=[
            pltpu.VMEM((SSEP, SSEP), jnp.float32),
            pltpu.VMEM((SSEP, BLK), jnp.float32),
        ],
        compiler_params=pltpu.CompilerParams(vmem_limit_bytes=VMEM_LIMIT),
        name="separator_front",
    )(jnp.stack([leaf_index, panel_index]), whole, shifts[None])
    return (factor_cols, coupling_cols, result_rows)


def solution(mesh):
    placed = (P("leaf", "panel"), P(), P(), P(), P(), P("panel"))
    return jax.shard_map(
        per_device,
        mesh=mesh,
        in_specs=placed,
        out_specs=(P("leaf", "panel"), P("leaf", "panel"), P("leaf", "panel")),
        check_vma=False,
    )
```

time: 716 us -> 772 us (1.078)
  waiting for transfers between devices: 257 us -> 584 us
  other arithmetic: 307 us -> 3.99 us
  Pallas kernels: 0 us -> 89 us
  blocking collectives: 0 us -> 73.6 us
  matrix products: 48.5 us -> 0 us
  local copies, waits for them, and re-layouts: 41.5 us -> 3.59 us
  starting transfers between devices: 28.5 us -> 0.12 us
  between operations: 26.2 us -> 17.7 us
    psum x0 -> x1, waiting for transfers between devices: none -> 535 us  [per_device(): summed = lax.psum(blocks, 'leaf')]
    another operation x49 -> x1, other arithmetic: 293 us -> 0.55 us  [per_device(): jnp.stack([leaf_index, panel_index])]
    ppermute x6 -> x0, waiting for transfers between devices: 179 us -> none  [partner(): lax.ppermute(array, axis, [(i, i ^ 1 << distance) for i in range(lax.axis...]
    pallas_call x0 -> x2, Pallas kernels: none -> 89 us  [the longest x1 50.6 us: per_device(): pl.pallas_call(separator_kernel, out_shape=jax.ShapeDtypeStruct((SSEP //...]
    all_gather x0 -> x1, blocking collectives: none -> 38.9 us  [per_device(): shifts = lax.all_gather(separator_shift, 'panel', axis=0, tiled=True)]
    all_to_all x0 -> x1, blocking collectives: none -> 34.7 us  [per_device(): lax.all_to_all(outgoing.reshape(rows, piece), 'leaf', split_axis=0, conca...]
    another operation x27 -> x0, matrix products: 34.5 us -> none  [the longest x14 23.1 us: per_device(): jnp.linalg.cholesky(whole)]
    all_to_all x1 -> x0, waiting for transfers between devices: 18.7 us -> none  [per_device(): lax.all_to_all(outgoing.reshape(rows_local, cols_local), 'leaf', split_ax...]
  transfers between devices with their start and end apart: 9 -> 3, of which waited for: 9 -> 3; matrix products, arithmetic and copies ran while one was open for 2% -> 1% of each run, Pallas kernels for 0% -> 0%
where the time goes in v1:
time: 772 us
  waiting for transfers between devices  584 us (76%)
  Pallas kernels  89 us (12%)
  blocking collectives  73.6 us (10%)
  between operations  17.7 us (2%)
    psum x1, waiting for transfers between devices, per_device(): summed = lax.psum(blocks, 'leaf')  535 us
    pallas_call x1, Pallas kernels, per_device(): pl.pallas_call(separator_kernel, out_shape=jax.ShapeDtypeStruct((SSEP //...  50.6 us
    all_gather x1, blocking collectives, per_device(): shifts = lax.all_gather(separator_shift, 'panel', axis=0, tiled=True)  38.9 us
    pallas_call x1, Pallas kernels, per_device(): pl.pallas_call(leaf_kernel, out_shape=(jax.ShapeDtypeStruct((KSUP, KSUP /...  38.4 us
    all_to_all x1, blocking collectives, per_device(): lax.all_to_all(outgoing.reshape(rows, piece), 'leaf', split_axis=0, conca...  34.7 us
    all_gather x1, waiting for transfers between devices, per_device(): design = lax.all_gather(received, 'panel', axis=0)  25.8 us
    all_gather x1, waiting for transfers between devices, per_device(): whole = lax.all_gather(summed, 'panel', axis=0)  23.2 us
  transfers between devices with their start and end apart: 3, of which 3 were waited for; matrix products, arithmetic and copies ran while one was open for 1% of the time, Pallas kernels for 0%

profile of v1, /device:TPU:1, one launch (start us, length us, event | category | flops | bytes accessed | tf_op | source)
XLA Modules:
  0.0 771.8 jit_solution(3845390592232991728)
XLA Ops:
  7.2 0.0 copy-start
  7.2 0.0 copy-start.2
  7.2 0.0 all-gather.4.cloned.1.call-start
  7.2 0.7 compare_select_fusion
  8.0 0.7 compare_and_fusion
  8.6 0.0 copy-done
  8.6 0.7 gather_fusion
  9.4 0.2 broadcast_select_fusion
  9.5 0.0 copy-start.1
  9.6 34.7 %all_to_all.6 = bf16[64,16,384]{2,1,0:T(8,128)(2,1)} all-to-all(bf16[64,16,384]{2,1,0:T(8,128)(2,1)S(1)} %broadcast_select_fusion), channel_id=1, replica_groups=mesh['leaf'=64,'panel'=4] {'leaf'}, dimensions={0} | all-to-all | bytes 1572864 | tf_op jit(solution)/shard_map/all_to_all | solution.py:237
  44.3 0.0 all-gather.4.cloned.1.call-update
  44.3 0.0 all-reduce.3.cloned.1.call-start
  44.3 0.0 copy-done.2
  44.4 0.6 dynamic_slice.12
  48.2 0.8 constant_dynamic-slice_fusion.1
  49.0 0.1 copy.11
  49.7 0.6 pad_convert_fusion.pattern
  50.3 1.3 fusion.2
  51.6 1.4 constant_dynamic-slice_fusion.shift
  53.0 25.8 %all-gather.4.cloned.1.call-done.design = bf16[4,1024,384]{2,1,0:T(8,128)(2,1)} async-done(((bf16[1,1024,384]{2,1,0:T(8,128)(2,1)}), bf16[4,1024,384]{2,1,0:T(8,128)(2,1)}) %all-gather.4.cloned.1.call-update) | async-done | bytes 3145744 | tf_op jit(solution)/shard_map/all_gather | solution.py:240
  78.8 38.4 %leaf_front.1 = (f32[512,128]{1,0:T(8,128)}, f32[1024,128]{1,0:T(8,128)}, f32[1152,128]{1,0:T(8,128)}) custom-call(s32[1]{0:T(128)} %bitcast.spot, bf16[4,1024,384]{2,1,0:T(8,128)(2,1)} %all-gather.4.cloned.1.call-done.design, s32[1,1024]{1,0:T(1,128)} %bitcast.13, f32[8,128]{1,0:T(8,128)} %pad_convert_fusion.pattern, f32[1,1536]{1,0:T(1,128)} %constant_dynamic-slice_fusion.shift), custom_call_target="tpu_custom_call" | custom-call | tf_op jit(solution)/shard_map/leaf_front/pallas_call | solution.py:248
  117.2 0.0 all-reduce.3.cloned.1.call-update
  117.2 0.0 all-gather.6.cloned.1.call-start
  117.3 534.6 %all-reduce.3.cloned.1.call-done = f32[1,1152,128]{2,1,0:T(8,128)} async-done(((f32[1,1152,128]{2,1,0:T(8,128)}), f32[1,1152,128]{2,1,0:T(8,128)}) %all-reduce.3.cloned.1.call-update) | async-done | bytes 589840 | tf_op jit(solution)/shard_map/psum | solution.py:266
  651.9 0.0 all-gather.6.cloned.1.call-update
  651.9 0.0 copy-done.1
  651.9 38.9 %all-gather = f32[4,1,256]{2,1,0:T(1,128)} all-gather(f32[1,1,256]{2,1,0:T(1,128)S(1)} %bitcast.14), channel_id=1, replica_groups=mesh['leaf'=64,'panel'=4] {'panel'}, dimensions={0}, use_global_device_ids=true | all-gather | bytes 5120 | tf_op jit(solution)/shard_map/all_gather | solution.py:268
  690.8 0.6 pad_add_fusion.spot
  691.4 23.2 %all-gather.6.cloned.1.call-done.blocks = f32[4,1152,128]{2,1,0:T(8,128)} async-done(((f32[1,1152,128]{2,1,0:T(8,128)}), f32[4,1152,128]{2,1,0:T(8,128)}) %all-gather.6.cloned.1.call-update) | async-done | bytes 2359312 | tf_op jit(solution)/shard_map/all_gather | solution.py:267
  714.6 50.6 %separator_front.1 = f32[16,256]{1,0:T(8,128)} custom-call(s32[2]{0:T(128)} %pad_add_fusion.spot, f32[4,1152,128]{2,1,0:T(8,128)} %all-gather.6.cloned.1.call-done.blocks, f32[1,1024]{1,0:T(1,128)} %bitcast.12), custom_call_target="tpu_custom_call" | custom-call | tf_op jit(solution)/shard_map/separator_front/pallas_call | solution.py:269
  (1 shorter events, 0.0 us)
Async XLA Ops:
  7.2 1.5 copy-start
  7.2 37.2 %copy-start.2 = (s32[64]{0:T(128)S(1)}, s32[64]{0:T(128)}, u32[]{:S(2)}) copy-start(s32[64]{0:T(128)} %param.8) | copy-start | bytes 772
  7.2 71.6 %all-gather.4.cloned.1.call-start = ((), (), s32[]{:S(2)}) async-start(), calls=%async_computation.1 | async-start | bytes 3932160 | tf_op jit(solution)/shard_map/all_gather | solution.py:240
  9.5 642.4 %copy-start.1 = (f32[256]{0:T(256)S(1)}, f32[256]{0:T(256)}, u32[]{:S(2)}) copy-start(f32[256]{0:T(256)} %param.11) | copy-start | bytes 3076
  44.3 607.6 %all-reduce.3.cloned.1.call-start = ((), (), s32[]{:S(2)}) async-start(), calls=%async_computation.2 | async-start | bytes 1179648 | tf_op jit(solution)/shard_map/psum | solution.py:266
  117.2 597.4 %all-gather.6.cloned.1.call-start = ((), (), s32[]{:S(2)}) async-start(), calls=%async_computation.3 | async-start | bytes 2949120 | tf_op jit(solution)/shard_map/all_gather | solution.py:267
Sparse Core Ops, SparseCore 0:
  44.4 34.3 all-gather.3
  117.3 534.5 all-reduce.2
  653.7 60.8 all-gather.5

commit v2 on v1

--- a/solution.py
+++ b/solution.py
@@ -205,7 +205,7 @@
             i = c if r == p else p + 1 + c
             value = blocks[p, i * BLK : (i + 1) * BLK, :] * share
             if c == r:
-                value = value + jnp.where(row_ids == col_ids, shift[0:1, span[1]], 0.0)
+                value = value + jnp.where(row_ids == col_ids, shift[r // 2, r % 2 : r % 2 + 1, :], 0.0)
             matrix[span] = value
     strips = [(t, t + 256, t + 256) for t in range(0, SSEP, 256)]
 
@@ -221,6 +221,311 @@
 
 VM = pl.BlockSpec(memory_space=pltpu.VMEM)
 SM = pl.BlockSpec(memory_space=pltpu.SMEM)
+MESH = pl.DeviceIdType.MESH
+Z, X, Y, LO = 8, 4, 4, 2
+
+
+def place():
+    leaf = lax.axis_index("leaf")
+    panel = lax.axis_index("panel")
+    z = leaf // (X * LO)
+    x = leaf // LO % X
+    y = panel // 2 * LO + leaf % LO
+    return z, x, y, panel % 2
+
+
+def device_at(z, x, y, core):
+    return ((z * X + x) * LO + y % LO, y // LO * 2 + core)
+
+
+def copy_to(source, target, sent, landed, device):
+    return pltpu.make_async_remote_copy(
+        src_ref=source, dst_ref=target, send_sem=sent, recv_sem=landed, device_id=device, device_id_type=MESH
+    )
+
+
+def greet(devices):
+    barrier = pltpu.get_barrier_semaphore()
+    for device in devices:
+        pl.semaphore_signal(barrier, inc=1, device_id=device, device_id_type=MESH)
+    pl.semaphore_wait(barrier, len(devices))
+
+
+TILES = 18
+STARTS = [15 * i // 7 for i in range(Z)]
+
+
+def sum_kernel(
+    blocks, shift, whole, shifts,
+    landed_a, partial, landed_b, reduced, gathered,
+    sent_a, got_a, sent_b, got_b, sent_c, got_c, local,
+    sent_1, got_1, sent_2, got_2, sent_s, got_s, sent_h, got_h,
+):
+    z, x, y, core = place()
+    lo, hi = y % LO, y // LO
+    piece = TILES * 8
+    half = piece // 2
+    plane = [(dx, dy) for dx in range(X) for dy in range(LO) if dx or dy]
+
+    def at_plane(dx, dy):
+        return device_at(z, (x + dx) % X, hi * LO + (lo + dy) % LO, core)
+
+    def at_z(d):
+        return device_at((z + d) % Z, x, y, core)
+
+    def at_y(d):
+        return device_at(z, x, (y + d) % Y, core)
+
+    def at_x(d):
+        return device_at(z, (x + d) % X, y, core)
+
+    sibling = device_at(z, x, y, 1 - core)
+    greet(
+        [at_plane(*d) for d in plane]
+        + [at_z(d) for d in range(1, Z)]
+        + [at_y(d) for d in range(1, Y)]
+        + [sibling]
+    )
+    pending = []
+
+    def go(copy):
+        copy.start()
+        pending.append(copy)
+        return copy
+
+    def rows_of(x_at, y_at):
+        return pl.multiple_of((x_at * LO + y_at % LO) * piece, 8)
+
+    def panel_of(y_at, core_at):
+        return y_at // LO * 2 + core_at
+
+    own_panel = panel_of(y, core)
+    go(copy_to(shift, shifts.at[own_panel], sent_h.at[0], got_h.at[0], at_y(2)))
+    go(copy_to(shift, shifts.at[own_panel], sent_h.at[1], got_h.at[1], sibling))
+    keep = pltpu.make_async_copy(shift, shifts.at[own_panel], local.at[Z])
+    keep.start()
+
+    first = []
+    for dx, dy in plane:
+        i = dx * LO + dy
+        at = rows_of((x + dx) % X, lo + dy)
+        first.append(
+            go(copy_to(blocks.at[pl.ds(at, piece), :], landed_a.at[i], sent_a.at[i], got_a.at[i], at_plane(dx, dy)))
+        )
+    total = blocks[pl.ds(rows_of(x, lo), piece), :]
+    for (dx, dy), copy in zip(plane, first):
+        copy.wait_recv()
+        total = total + landed_a[dx * LO + dy]
+    partial[...] = total
+
+    def start_of(z_at):
+        return pl.multiple_of(15 * z_at // 7 * 8, 8)
+
+    second = []
+    for d in range(1, Z):
+        source = partial.at[pl.ds(start_of((z + d) % Z), 24), :]
+        second.append(go(copy_to(source, landed_b.at[d], sent_b.at[d], got_b.at[d], at_z(d))))
+    total = partial[pl.ds(start_of(z), 24), :]
+    for d, copy in zip(range(1, Z), second):
+        copy.wait_recv()
+        total = total + landed_b[d]
+    reduced[...] = total
+
+    third = [
+        go(copy_to(reduced, gathered.at[z], sent_c.at[d], got_c.at[d], at_z(d))) for d in range(1, Z)
+    ]
+    mine = pltpu.make_async_copy(reduced, gathered.at[z], local.at[0])
+    mine.start()
+    pending[0].wait_recv()
+    go(copy_to(shifts.at[panel_of(y + 2 - y // 2 * 4, core)], shifts.at[panel_of(y + 2 - y // 2 * 4, core)],
+               sent_h.at[2], got_h.at[2], sibling))
+    mine.wait()
+    for copy in third:
+        copy.wait_recv()
+    top = rows_of(x, y)
+    own = whole.at[own_panel, pl.ds(top, piece), :]
+    moves = []
+    for i in range(Z):
+        length = ((STARTS + [TILES])[i + 1] - STARTS[i]) * 8
+        move = pltpu.make_async_copy(
+            gathered.at[i, 0:length, :],
+            whole.at[own_panel, pl.ds(pl.multiple_of(top + STARTS[i] * 8, 8), length), :],
+            local.at[i],
+        )
+        move.start()
+        moves.append(move)
+    for move in moves:
+        move.wait()
+
+    def part(x_at, y_at, side, core_at=core):
+        at = pl.multiple_of(rows_of(x_at, y_at) + side * half, 8)
+        return whole.at[panel_of(y_at, core_at), pl.ds(at, half), :]
+
+    def pass_on(ref, sems_sent, sems_got, index, device):
+        return go(copy_to(ref, ref, sems_sent.at[index], sems_got.at[index], device))
+
+    ring = [at_y, at_x]
+    length = Y
+    first_wave = {}
+    for side in range(2):
+        for d in range(1, length):
+            first_wave[side, d] = pass_on(part(x, y, side), sent_1, got_1, side * 4 + d, ring[side](d))
+    second_wave = []
+
+    def spread(side, d):
+        where = part(x, (y - d) % Y, 0) if side == 0 else part((x - d) % X, y, 1)
+        for e in range(1, length):
+            second_wave.append(
+                (side, d, e, pass_on(where, sent_2, got_2, (side * 4 + d) * 4 + e, ring[1 - side](e)))
+            )
+        pass_on(where, sent_s, got_s, (side * 4 + d) * 4, sibling)
+
+    for side in range(2):
+        spread(side, 0)
+    for d in range(1, length):
+        for side in range(2):
+            first_wave[side, d].wait_recv()
+            spread(side, d)
+    for side, d, e, copy in second_wave:
+        copy.wait_recv()
+        if side == 0:
+            where = part((x - e) % X, (y - d) % Y, 0)
+        else:
+            where = part((x - d) % X, (y - e) % Y, 1)
+        pass_on(where, sent_s, got_s, (side * 4 + d) * 4 + e, sibling)
+    for copy in pending:
+        copy.wait_send()
+    for side in range(2):
+        for d in range(length):
+            for e in range(length):
+                if side == 0:
+                    where = part((x - e) % X, (y - d) % Y, 0, 1 - core)
+                else:
+                    where = part((x - d) % X, (y - e) % Y, 1, 1 - core)
+                index = (side * 4 + d) * 4 + e
+                copy_to(where, where, sent_s.at[index], got_s.at[index], sibling).wait_recv()
+    keep.wait()
+    for i, panel in ((1, panel_of(y, 1 - core)), (2, panel_of(y + 2 - y // 2 * 4, 1 - core))):
+        copy_to(shift, shifts.at[panel], sent_h.at[i], got_h.at[i], sibling).wait_recv()
+
+
+def sum_blocks(blocks, shift):
+    rows = blocks.shape[0]
+    dma = pltpu.SemaphoreType.DMA
+    f32 = jnp.float32
+    return pl.pallas_call(
+        sum_kernel,
+        out_shape=(
+            jax.ShapeDtypeStruct((4, rows, BLK), f32),
+            jax.ShapeDtypeStruct((4, 2, BLK), f32),
+        ),
+        in_specs=[VM, VM],
+        out_specs=(VM, VM),
+        scratch_shapes=[
+            pltpu.VMEM((8, TILES * 8, BLK), f32),
+            pltpu.VMEM((TILES * 8, BLK), f32),
+            pltpu.VMEM((Z, 24, BLK), f32),
+            pltpu.VMEM((24, BLK), f32),
+            pltpu.VMEM((Z, 24, BLK), f32),
+            dma((8,)), dma((8,)), dma((8,)), dma((8,)), dma((8,)), dma((8,)), dma((Z + 1,)),
+            dma((8,)), dma((8,)), dma((32,)), dma((32,)), dma((32,)), dma((32,)), dma((3,)), dma((3,)),
+        ],
+        compiler_params=pltpu.CompilerParams(collective_id=1, has_side_effects=True, vmem_limit_bytes=40 << 20),
+        name="separator_sum",
+    )(blocks, shift)
+
+
+ORDER = (0, 1, 7, 2, 6, 3, 5, 4)
+
+
+def relay(along, dz, slab, go, sent_s, got_s, sibling):
+    for d in (1, 3, 2):
+        along[dz, d].wait_recv()
+        i = dz * Y + d
+        go(copy_to(slab(dz, d), slab(dz, d), sent_s.at[i], got_s.at[i], sibling))
+
+
+def exchange_kernel(outgoing, design, middle, local, sent_a, got_a, sent_y, got_y, sent_s, got_s):
+    z, x, y, core = place()
+    own_panel = y // LO * 2 + core
+    sibling = device_at(z, x, y, 1 - core)
+    near = [(dz, dx) for dz in ORDER for dx in range(X) if dz or dx]
+
+    def at(dz, dx):
+        return device_at((z + dz) % Z, (x + dx) % X, y, core)
+
+    def at_y(d):
+        return device_at(z, x, (y + d) % Y, core)
+
+    greet([at(*d) for d in near] + [at_y(d) for d in range(1, Y)] + [sibling])
+    pending = []
+
+    def go(copy):
+        copy.start()
+        pending.append(copy)
+        return copy
+
+    arrive = {}
+    keep = pltpu.make_async_copy(outgoing.at[z, x], middle.at[z, x], local.at[Z])
+    keep.start()
+    for dz, dx in near:
+        i = dz * X + dx
+        arrive[dz, dx] = go(
+            copy_to(
+                outgoing.at[(z + dz) % Z, (x + dx) % X], middle.at[z, x], sent_a.at[i], got_a.at[i], at(dz, dx)
+            )
+        )
+    along = {}
+    moves = []
+
+    def slab(dz, d):
+        y_from = (y - d) % Y
+        return design.at[y_from // LO * 2 + core, (z - dz) % Z, :, y_from % LO]
+
+    for n, dz in enumerate(ORDER):
+        for dx in range(X):
+            if dz or dx:
+                arrive[dz, dx].wait_recv()
+        if dz == 0:
+            keep.wait()
+        z_from = (z - dz) % Z
+        target = design.at[own_panel, z_from, :, y % LO]
+        other = middle.at[z_from, :, 1 - y % LO]
+        same = middle.at[z_from, :, y % LO]
+        for d in (2, 1, 3):
+            source = same if d == 2 else other
+            i = dz * Y + d
+            along[dz, d] = go(copy_to(source, target, sent_y.at[i], got_y.at[i], at_y(d)))
+        go(copy_to(same, target, sent_s.at[dz * Y], got_s.at[dz * Y], sibling))
+        move = pltpu.make_async_copy(same, target, local.at[dz])
+        move.start()
+        moves.append(move)
+        if n:
+            relay(along, ORDER[n - 1], slab, go, sent_s, got_s, sibling)
+    relay(along, ORDER[-1], slab, go, sent_s, got_s, sibling)
+    for copy in pending:
+        copy.wait_send()
+    for move in moves:
+        move.wait()
+    for dz in ORDER:
+        for d in range(Y):
+            i = dz * Y + d
+            copy_to(slab(dz, d), slab(dz, d), sent_s.at[i], got_s.at[i], sibling).wait_recv()
+
+
+def exchange(outgoing):
+    dma = pltpu.SemaphoreType.DMA
+    rows, piece = outgoing.shape[-2:]
+    return pl.pallas_call(
+        exchange_kernel,
+        out_shape=jax.ShapeDtypeStruct((4,) + outgoing.shape, outgoing.dtype),
+        in_specs=[VM],
+        out_specs=VM,
+        scratch_shapes=[pltpu.VMEM(outgoing.shape, outgoing.dtype), dma((Z + 1,))]
+        + [dma((Z * X,)) for _ in range(6)],
+        compiler_params=pltpu.CompilerParams(collective_id=2, has_side_effects=True, vmem_limit_bytes=40 << 20),
+        name="design_exchange",
+    )(outgoing)
 
 
 def per_device(
@@ -234,10 +539,8 @@
     panel_index = lax.axis_index("panel")
     subtree = subtree_of[leaf_index]
     outgoing = jnp.take(pix_cycle.reshape(leaves, block_rows, piece), subtree_of, axis=0)
-    received = lax.all_to_all(
-        outgoing.reshape(rows, piece), "leaf", split_axis=0, concat_axis=0, tiled=True
-    )
-    design = lax.all_gather(received, "panel", axis=0)
+    received = exchange(outgoing.reshape(Z, X, LO, block_rows, piece))
+    design = received.reshape(panels, rows, piece)
     cycle_index = lax.dynamic_slice_in_dim(cycle_to_dissection, subtree * rows, rows)
     position = (cycle_index // rows) * block_rows + cycle_index % rows - subtree * block_rows
     row_blocks = rows // BLK
@@ -263,9 +566,7 @@
         compiler_params=pltpu.CompilerParams(vmem_limit_bytes=VMEM_LIMIT),
         name="leaf_front",
     )(panel_index[None], design, position[None], pattern, shift)
-    summed = lax.psum(blocks, "leaf")
-    whole = lax.all_gather(summed, "panel", axis=0)
-    shifts = lax.all_gather(separator_shift, "panel", axis=0, tiled=True)
+    whole, shifts = sum_blocks(blocks, separator_shift.reshape(2, BLK))
     result_rows = pl.pallas_call(
         separator_kernel,
         out_shape=jax.ShapeDtypeStruct((SSEP // leaves, SSEP // panels), jnp.float32),
@@ -277,7 +578,7 @@
         ],
         compiler_params=pltpu.CompilerParams(vmem_limit_bytes=VMEM_LIMIT),
         name="separator_front",
-    )(jnp.stack([leaf_index, panel_index]), whole, shifts[None])
+    )(jnp.stack([leaf_index, panel_index]), whole, shifts)
     return (factor_cols, coupling_cols, result_rows)
 
 

time: 772 us -> 186 us (0.24)
  waiting for transfers between devices: 584 us -> 0 us
  Pallas kernels: 89 us -> 168 us
  blocking collectives: 73.6 us -> 0 us
  between operations: 17.7 us -> 4.6 us
    psum x1 -> x0, waiting for transfers between devices: 535 us -> none  [per_device(): summed = lax.psum(blocks, 'leaf')]
    pallas_call x0 -> x2, Pallas kernels: none -> 79.2 us  [the longest x1 42.3 us: exchange(): pl.pallas_call(exchange_kernel, out_shape=jax.ShapeDtypeStruct((4,) + out...]
    all_gather x2 -> x0, waiting for transfers between devices: 49 us -> none  [the longest x1 25.8 us: per_device(): design = lax.all_gather(received, 'panel', axis=0)]
    all_gather x1 -> x0, blocking collectives: 38.9 us -> none  [per_device(): shifts = lax.all_gather(separator_shift, 'panel', axis=0, tiled=True)]
    all_to_all x1 -> x0, blocking collectives: 34.7 us -> none  [per_device(): lax.all_to_all(outgoing.reshape(rows, piece), 'leaf', split_axis=0, conca...]
  transfers between devices with their start and end apart: 3 -> 0, of which waited for: 3 -> 0; matrix products, arithmetic and copies ran while one was open for 1% -> 0% of each run, Pallas kernels for 0% -> 0%
where the time goes in v2:
time: 186 us
  Pallas kernels  168 us (90%)
  local copies, waits for them, and re-layouts  9.1 us (5%)
  between operations  4.6 us (2%)
  other arithmetic  4.02 us (2%)
    pallas_call x1, Pallas kernels, per_device(): pl.pallas_call(separator_kernel, out_shape=jax.ShapeDtypeStruct((SSEP //...  50.4 us
    pallas_call x1, Pallas kernels, exchange(): pl.pallas_call(exchange_kernel, out_shape=jax.ShapeDtypeStruct((4,) + out...  42.3 us
    pallas_call x1, Pallas kernels, per_device(): pl.pallas_call(leaf_kernel, out_shape=(jax.ShapeDtypeStruct((KSUP, KSUP /...  38.4 us
    pallas_call x1, Pallas kernels, sum_blocks(): pl.pallas_call(sum_kernel, out_shape=(jax.ShapeDtypeStruct((4, rows, BLK)...  36.9 us
    unnamed x13, local copies, waits for them, and re-layouts  4.79 us

profile of v2, /device:TPU:1, one launch (start us, length us, event | category | flops | bytes accessed | tf_op | source)
XLA Modules:
  0.0 185.8 jit_solution(7412502570846696491)
XLA Ops:
  0.6 0.0 copy-start
  0.6 1.3 dynamic_slice.12
  5.9 0.7 pad_add_fusion.spot
  6.5 0.0 copy-done
  6.5 0.7 compare_and_fusion
  7.2 0.7 compare_select_fusion
  7.8 1.3 fusion.2
  9.1 0.1 broadcast_in_dim.21
  9.2 1.4 constant_dynamic-slice_fusion.shift
  10.6 0.8 constant_dynamic-slice_fusion.1
  11.4 0.1 copy.11
  11.5 0.6 pad_convert_fusion.pattern
  12.1 0.7 gather_fusion
  12.8 0.2 broadcast_select_fusion.outgoing
  13.0 0.0 copy-start.5
  13.0 42.3 %design_exchange.1 = bf16[4,8,4,2,16,384]{5,4,3,2,1,0:T(8,128)(2,1)S(1)} custom-call(bf16[8,4,2,16,384]{4,3,2,1,0:T(8,128)(2,1)S(1)} %broadcast_select_fusion.outgoing), custom_call_target="tpu_custom_call" | custom-call | tf_op jit(solution)/shard_map/design_exchange/pallas_call | solution.py:519
  55.3 0.0 copy-start.1
  55.3 1.6 copy-done.1
  57.0 38.4 %leaf_front.1 = (f32[512,128]{1,0:T(8,128)}, f32[1024,128]{1,0:T(8,128)}, f32[1152,128]{1,0:T(8,128)}) custom-call(s32[1]{0:T(128)} %bitcast.spot, bf16[4,1024,384]{2,1,0:T(8,128)(2,1)} %bitcast.9, s32[1,1024]{1,0:T(1,128)} %bitcast.12, f32[8,128]{1,0:T(8,128)} %pad_convert_fusion.pattern, f32[1,1536]{1,0:T(1,128)} %constant_dynamic-slice_fusion.shift), custom_call_target="tpu_custom_call" | custom-call | tf_op jit(solution)/shard_map/leaf_front/pallas_call | solution.py:551
  95.4 0.0 copy-done.5
  95.4 0.0 copy-start.3
  95.4 1.1 copy-done.3
  96.4 36.9 %separator_sum.1 = (f32[4,1152,128]{2,1,0:T(8,128)S(1)}, f32[4,2,128]{2,1,0:T(2,128)S(1)}) custom-call(f32[1152,128]{1,0:T(8,128)S(1)} %copy-done.3, f32[2,128]{1,0:T(2,128)S(1)} %bitcast.10), custom_call_target="tpu_custom_call" | custom-call | tf_op jit(solution)/shard_map/separator_sum/pallas_call | solution.py:416
  133.4 0.0 copy-start.2
  133.4 1.4 copy-done.2
  134.8 0.0 copy-start.4
  134.8 0.6 copy-done.4
  135.4 50.4 %separator_front.1 = f32[16,256]{1,0:T(8,128)} custom-call(s32[2]{0:T(128)} %pad_add_fusion.spot, f32[4,1152,128]{2,1,0:T(8,128)} %copy-done.2, f32[4,2,128]{2,1,0:T(2,128)} %copy-done.4), custom_call_target="tpu_custom_call" | custom-call | tf_op jit(solution)/shard_map/separator_front/pallas_call | solution.py:570
  (1 shorter events, 0.0 us)
Async XLA Ops:
  0.6 5.9 %copy-start = (bf16[1024,384]{1,0:T(8,128)(2,1)S(1)}, bf16[1024,384]{1,0:T(8,128)(2,1)}, u32[]{:S(2)}) copy-start(bf16[1024,384]{1,0:T(8,128)(2,1)} %param.6) | copy-start | bytes 2359300
  13.0 82.4 %copy-start.5 = (f32[256]{0:T(256)S(1)}, f32[256]{0:T(256)}, u32[]{:S(2)}) copy-start(f32[256]{0:T(256)} %param.11) | copy-start | bytes 3076
  55.3 1.6 copy-start.1
  95.4 1.1 copy-start.3
  133.4 1.4 copy-start.2
  134.8 0.6 copy-start.4

commit v3 on v2

--- a/solution.py
+++ b/solution.py
@@ -69,7 +69,7 @@
                 solved[k] = solved[k] - mult[k, i] * solved[i]
         for b in range(s + 1, count):
             rest = jnp.where(inside, 0.0, work[b])
-            for k in range(SLAB):
+            for k in reversed(range(SLAB)):
                 rest = rest - below[b][k] * twice(solved[k])
             work[b] = rest
         out = jnp.zeros((SLAB, BLK), jnp.float32)
@@ -104,37 +104,47 @@
     return lax.dot_general(a, b, (((0,), (0,)), ((), ())), preferred_element_type=jnp.float32)
 
 
-def eliminate(matrix, panel_ref, at, strips):
+def split_parts(values):
+    high = values.astype(jnp.bfloat16)
+    rest = values - high.astype(jnp.float32)
+    middle = rest.astype(jnp.bfloat16)
+    low = (rest - middle.astype(jnp.float32)).astype(jnp.bfloat16)
+    left = jnp.concatenate([high, middle, high, middle, high, low], 1)
+    right = jnp.concatenate([high, high, middle, middle, low, high], 1)
+    return left, right
+
+
+def make_panel(matrix, inverse, factor, left, right, at):
     rows = matrix.shape[0]
-    factor, inverse = factor_block(matrix[pl.ds(at, BLK), pl.ds(at, BLK)])
     panel = dot_nt(matrix[:, pl.ds(at, BLK)], inverse)
     row_ids = lax.broadcasted_iota(jnp.int32, (rows, BLK), 0)
     panel = jnp.where(row_ids >= at + BLK, panel, 0.0)
-    panel_ref[...] = panel
+    left[...], right[...] = split_parts(panel)
     matrix[:, pl.ds(at, BLK)] = panel
     matrix[pl.ds(at, BLK), pl.ds(at, BLK)] = factor
+
+
+def next_block(matrix, inverse, at):
+    after = pl.multiple_of(at + BLK, BLK)
+    head = dot_nt(matrix[pl.ds(after, BLK), pl.ds(at, BLK)], inverse)
+    return matrix[pl.ds(after, BLK), pl.ds(after, BLK)] - dot_nt(head, head)
+
+
+def subtract(matrix, left, right, strips):
     for top, bottom, width in strips:
-
-        @pl.when(width > at + BLK)
-        def _():
-            matrix[top:bottom, :width] = matrix[top:bottom, :width] - dot_nt(
-                panel_ref[top:bottom, :], panel_ref[:width, :]
-            )
+        matrix[top:bottom, :width] = matrix[top:bottom, :width] - dot_nt(
+            left[top:bottom, :], right[:width, :], None
+        )
 
 
 def leaf_kernel(
-    spot, design, position, pattern, shift, factor_out, coupling_out, blocks_out,
-    masked, front, panel_ref, trail,
+    spot, design, touch, shift_rows, factor_out, coupling_out, blocks_out,
+    masked, front, left, right, trail, inverse_ref, factor_ref, shift,
 ):
     panel_index = spot[0]
     rows = design.shape[1]
     piece = design.shape[2]
-    here = lax.broadcasted_iota(jnp.int32, (rows, rows), 0)
-    chosen = jnp.where(here == position[0:1, :], 1.0, 0.0).astype(jnp.bfloat16)
-    fill = jnp.concatenate(
-        [jnp.broadcast_to(pattern[b : b + 1, :], (BLK, BLK)) for b in range(rows // BLK)], 0
-    )
-    touch = jnp.dot(chosen, fill.astype(jnp.bfloat16), preferred_element_type=jnp.float32)
+    shift[...] = shift_rows[pl.ds(spot[1], 1), :]
     for c in range(FRONT // BLK):
         p, at = c * BLK // piece, c * BLK % piece
         keep = jnp.broadcast_to(touch[:, c : c + 1], (rows, BLK)).astype(jnp.bfloat16)
@@ -147,7 +157,7 @@
     same = row_ids == col_ids
     for b in range(KSUP // BLK):
         span = slice(b * BLK, (b + 1) * BLK)
-        front[span, span] = front[span, span] + jnp.where(same, shift[0:1, span], 0.0)
+        front[span, span] = front[span, span] + jnp.where(same, shift[:, span], 0.0)
     last = SSEP // BLK - 1
     halves = (panel_index, last - panel_index)
     for h, block_row in enumerate(halves):
@@ -157,40 +167,47 @@
         )
         corner = pl.ds(pl.multiple_of(block_row * BLK, BLK), BLK)
         span = slice(h * BLK, (h + 1) * BLK)
-        trail[span, corner] = trail[span, corner] + jnp.where(same, shift[0:1, pl.ds(at, BLK)], 0.0)
-
-    strips = [(0, 256, 256), (256, FRONT, KSUP)]
+        line = shift[:, pl.ds(at, BLK)]
+        trail[span, corner] = trail[span, corner] + jnp.where(same, line, 0.0)
+
+    def subtract_trail():
+        for h, block_row in enumerate(halves):
+            at = pl.multiple_of(KSUP + block_row * BLK, BLK)
+            span = slice(h * BLK, (h + 1) * BLK)
+            trail[span, :] = trail[span, :] - dot_nt(left[pl.ds(at, BLK), :], right[KSUP:, :], None)
+
+    factor_ref[...], inverse_ref[...] = factor_block(front[:BLK, :BLK])
 
     def step(j, carry):
         at = pl.multiple_of(j * BLK, BLK)
-        eliminate(front, panel_ref, at, strips)
-
-        @pl.when(j == panel_index)
-        def _():
-            factor_out[...] = front[:KSUP, pl.ds(at, BLK)]
-            coupling_out[...] = front[KSUP:, pl.ds(at, BLK)]
-
+        inverse = inverse_ref[...]
+        block = next_block(front, inverse, at)
+        make_panel(front, inverse, factor_ref[...], left, right, at)
+        subtract(front, left, right, [(BLK, 256, 256), (256, FRONT, KSUP)])
+        subtract_trail()
+        factor_ref[...], inverse_ref[...] = factor_block(block)
         return carry
 
-    lax.fori_loop(0, KSUP // BLK, step, 0)
-    for h, block_row in enumerate(halves):
-        at = pl.multiple_of(KSUP + block_row * BLK, BLK)
-        span = slice(h * BLK, (h + 1) * BLK)
-        trail[span, :] = trail[span, :] - dot_nt(front[pl.ds(at, BLK), :], front[KSUP:, :])
+    lax.fori_loop(0, KSUP // BLK - 1, step, 0)
+    make_panel(front, inverse_ref[...], factor_ref[...], left, right, KSUP - BLK)
+    subtract_trail()
+    mine = pl.ds(pl.multiple_of(panel_index * BLK, BLK), BLK)
+    factor_out[...] = front[:KSUP, mine]
+    coupling_out[...] = front[KSUP:, mine]
 
     def pack(i, carry):
         second = i > panel_index
         top = pl.multiple_of(jnp.where(second, BLK, 0), BLK)
-        left = pl.multiple_of(jnp.where(second, i - panel_index - 1, i) * BLK, BLK)
+        start = pl.multiple_of(jnp.where(second, i - panel_index - 1, i) * BLK, BLK)
         blocks_out[pl.ds(pl.multiple_of(i * BLK, BLK), BLK), :] = trail[
-            pl.ds(top, BLK), pl.ds(left, BLK)
+            pl.ds(top, BLK), pl.ds(start, BLK)
         ]
         return carry
 
     lax.fori_loop(0, last + 2, pack, 0)
 
 
-def separator_kernel(spot, blocks, shift, out, matrix, panel_ref):
+def separator_kernel(spot, blocks, shift, out, matrix, left, right, inverse_ref, factor_ref):
     size = SSEP // BLK
     share = 1.0 / 64
     row_ids = lax.broadcasted_iota(jnp.int32, (BLK, BLK), 0)
@@ -205,18 +222,42 @@
             i = c if r == p else p + 1 + c
             value = blocks[p, i * BLK : (i + 1) * BLK, :] * share
             if c == r:
-                value = value + jnp.where(row_ids == col_ids, shift[r // 2, r % 2 : r % 2 + 1, :], 0.0)
+                line = shift[r // 2, r % 2 : r % 2 + 1, :]
+                value = value + jnp.where(row_ids == col_ids, line, 0.0)
             matrix[span] = value
     strips = [(t, t + 256, t + 256) for t in range(0, SSEP, 256)]
+    factor_ref[...], inverse_ref[...] = factor_block(matrix[:BLK, :BLK])
 
     def step(j, carry):
-        eliminate(matrix, panel_ref, pl.multiple_of(j * BLK, BLK), strips)
+        at = pl.multiple_of(j * BLK, BLK)
+        inverse = inverse_ref[...]
+        block = next_block(matrix, inverse, at)
+        make_panel(matrix, inverse, factor_ref[...], left, right, at)
+        subtract(matrix, left, right, strips)
+        factor_ref[...], inverse_ref[...] = factor_block(block)
         return carry
 
-    lax.fori_loop(0, size, step, 0)
+    lax.fori_loop(0, size - 1, step, 0)
+    matrix[: SSEP - BLK, SSEP - BLK :] = jnp.zeros((SSEP - BLK, BLK), jnp.float32)
+    matrix[SSEP - BLK :, SSEP - BLK :] = factor_ref[...]
     top = pl.multiple_of(spot[0] * out.shape[0], out.shape[0])
-    left = pl.multiple_of(spot[1] * out.shape[1], out.shape[1])
-    out[...] = matrix[pl.ds(top, out.shape[0]), pl.ds(left, out.shape[1])]
+    start = pl.multiple_of(spot[1] * out.shape[1], out.shape[1])
+    out[...] = matrix[pl.ds(top, out.shape[0]), pl.ds(start, out.shape[1])]
+
+
+def start_kernel(spot, subtree_of, design, cycle_index, outgoing, position, subtree_out):
+    leaves, block_rows, _ = design.shape
+    rows = leaves * block_rows
+    subtree = subtree_of[spot[0]]
+    subtree_out[0] = subtree
+    index = cycle_index[pl.ds(pl.multiple_of(subtree * 8, 8), 8), :]
+    position[...] = (index // rows) * block_rows + index % rows - subtree * block_rows
+
+    def move(d, carry):
+        outgoing[d] = design[subtree_of[d]]
+        return carry
+
+    lax.fori_loop(0, leaves, move, 0, unroll=8)
 
 
 VM = pl.BlockSpec(memory_space=pltpu.VMEM)
@@ -445,7 +486,25 @@
         go(copy_to(slab(dz, d), slab(dz, d), sent_s.at[i], got_s.at[i], sibling))
 
 
-def exchange_kernel(outgoing, design, middle, local, sent_a, got_a, sent_y, got_y, sent_s, got_s):
+def row_pattern(subtree, position, fill):
+    count, lanes = position.shape
+    rows = count * lanes
+    here = lax.broadcasted_iota(jnp.int32, (rows, lanes), 0)
+    chosen = jnp.concatenate(
+        [jnp.where(here == position[b : b + 1, :], 1.0, 0.0) for b in range(count)], 1
+    ).astype(jnp.bfloat16)
+    blocks = fill.shape[1]
+    source = lax.broadcasted_iota(jnp.int32, (blocks, rows), 0)
+    wanted = subtree * count + lax.broadcasted_iota(jnp.int32, (blocks, rows), 1) // lanes
+    pick = jnp.where(source == wanted, 1.0, 0.0).astype(jnp.bfloat16)
+    lines = jnp.dot(fill[...].astype(jnp.bfloat16), pick, preferred_element_type=jnp.float32)
+    return dot_nt(chosen, lines.astype(jnp.bfloat16), None)
+
+
+def exchange_kernel(
+    outgoing, position, subtree, fill, design, touch,
+    middle, local, sent_a, got_a, sent_y, got_y, sent_s, got_s,
+):
     z, x, y, core = place()
     own_panel = y // LO * 2 + core
     sibling = device_at(z, x, y, 1 - core)
@@ -475,6 +534,7 @@
                 outgoing.at[(z + dz) % Z, (x + dx) % X], middle.at[z, x], sent_a.at[i], got_a.at[i], at(dz, dx)
             )
         )
+    touch[...] = row_pattern(subtree[0], position[...], fill)
     along = {}
     moves = []
 
@@ -513,19 +573,22 @@
             copy_to(slab(dz, d), slab(dz, d), sent_s.at[i], got_s.at[i], sibling).wait_recv()
 
 
-def exchange(outgoing):
+def exchange(outgoing, position, subtree, fill):
     dma = pltpu.SemaphoreType.DMA
     rows, piece = outgoing.shape[-2:]
     return pl.pallas_call(
         exchange_kernel,
-        out_shape=jax.ShapeDtypeStruct((4,) + outgoing.shape, outgoing.dtype),
-        in_specs=[VM],
-        out_specs=VM,
+        out_shape=(
+            jax.ShapeDtypeStruct((4,) + outgoing.shape, outgoing.dtype),
+            jax.ShapeDtypeStruct((position.size, fill.shape[0]), jnp.float32),
+        ),
+        in_specs=[VM, VM, SM, VM],
+        out_specs=(VM, VM),
         scratch_shapes=[pltpu.VMEM(outgoing.shape, outgoing.dtype), dma((Z + 1,))]
         + [dma((Z * X,)) for _ in range(6)],
         compiler_params=pltpu.CompilerParams(collective_id=2, has_side_effects=True, vmem_limit_bytes=40 << 20),
         name="design_exchange",
-    )(outgoing)
+    )(outgoing, position, subtree, fill)
 
 
 def per_device(
@@ -537,16 +600,27 @@
     block_rows = rows // leaves
     leaf_index = lax.axis_index("leaf")
     panel_index = lax.axis_index("panel")
-    subtree = subtree_of[leaf_index]
-    outgoing = jnp.take(pix_cycle.reshape(leaves, block_rows, piece), subtree_of, axis=0)
-    received = exchange(outgoing.reshape(Z, X, LO, block_rows, piece))
+    outgoing, position, subtree = pl.pallas_call(
+        start_kernel,
+        out_shape=(
+            jax.ShapeDtypeStruct((leaves, block_rows, piece), pix_cycle.dtype),
+            jax.ShapeDtypeStruct((8, BLK), jnp.int32),
+            jax.ShapeDtypeStruct((1,), jnp.int32),
+        ),
+        in_specs=[SM, SM, VM, VM],
+        out_specs=(VM, VM, SM),
+        compiler_params=pltpu.CompilerParams(vmem_limit_bytes=VMEM_LIMIT),
+        name="start_rows",
+    )(
+        leaf_index[None],
+        subtree_of,
+        pix_cycle.reshape(leaves, block_rows, piece),
+        cycle_to_dissection.reshape(-1, BLK),
+    )
+    received, touch = exchange(
+        outgoing.reshape(Z, X, LO, block_rows, piece), position, subtree, fill_blocks.T
+    )
     design = received.reshape(panels, rows, piece)
-    cycle_index = lax.dynamic_slice_in_dim(cycle_to_dissection, subtree * rows, rows)
-    position = (cycle_index // rows) * block_rows + cycle_index % rows - subtree * block_rows
-    row_blocks = rows // BLK
-    pattern = lax.dynamic_slice_in_dim(fill_blocks, subtree * row_blocks, row_blocks)
-    pattern = jnp.pad(pattern, ((0, 0), (0, BLK - pattern.shape[1]))).astype(jnp.float32)
-    shift = lax.dynamic_slice_in_dim(leaf_shift, subtree, 1, 0)
     count = SSEP // BLK + 1
     factor_cols, coupling_cols, blocks = pl.pallas_call(
         leaf_kernel,
@@ -555,17 +629,21 @@
             jax.ShapeDtypeStruct((SSEP, KSUP // panels), jnp.float32),
             jax.ShapeDtypeStruct((count * BLK, BLK), jnp.float32),
         ),
-        in_specs=[SM, VM, VM, VM, VM],
+        in_specs=[SM, VM, VM, VM],
         out_specs=(VM, VM, VM),
         scratch_shapes=[
             pltpu.VMEM((rows, FRONT), jnp.bfloat16),
             pltpu.VMEM((FRONT, KSUP), jnp.float32),
-            pltpu.VMEM((FRONT, BLK), jnp.float32),
+            pltpu.VMEM((FRONT, 6 * BLK), jnp.bfloat16),
+            pltpu.VMEM((FRONT, 6 * BLK), jnp.bfloat16),
             pltpu.VMEM((2 * BLK, SSEP), jnp.float32),
+            pltpu.VMEM((BLK, BLK), jnp.float32),
+            pltpu.VMEM((BLK, BLK), jnp.float32),
+            pltpu.VMEM((1, FRONT), jnp.float32),
         ],
         compiler_params=pltpu.CompilerParams(vmem_limit_bytes=VMEM_LIMIT),
         name="leaf_front",
-    )(panel_index[None], design, position[None], pattern, shift)
+    )(jnp.stack([panel_index, subtree[0]]), design, touch, leaf_shift)
     whole, shifts = sum_blocks(blocks, separator_shift.reshape(2, BLK))
     result_rows = pl.pallas_call(
         separator_kernel,
@@ -574,7 +652,10 @@
         out_specs=VM,
         scratch_shapes=[
             pltpu.VMEM((SSEP, SSEP), jnp.float32),
-            pltpu.VMEM((SSEP, BLK), jnp.float32),
+            pltpu.VMEM((SSEP, 6 * BLK), jnp.bfloat16),
+            pltpu.VMEM((SSEP, 6 * BLK), jnp.bfloat16),
+            pltpu.VMEM((BLK, BLK), jnp.float32),
+            pltpu.VMEM((BLK, BLK), jnp.float32),
         ],
         compiler_params=pltpu.CompilerParams(vmem_limit_bytes=VMEM_LIMIT),
         name="separator_front",

time: 186 us -> 155 us (0.83)
  Pallas kernels: 168 us -> 145 us
  between operations: 4.6 us -> 0.69 us
  other arithmetic: 4.02 us -> 1.27 us
    pallas_call x1, Pallas kernels: 50.4 us -> 36.2 us  [per_device(): pl.pallas_call(separator_kernel, out_shape=jax.ShapeDtypeStruct((SSEP //...]
    pallas_call x1, Pallas kernels: 38.4 us -> 26.6 us  [per_device(): pl.pallas_call(leaf_kernel, out_shape=(jax.ShapeDtypeStruct((KSUP, KSUP /...]
    dynamic_slice x3 -> x0, local copies, waits for them, and re-layouts: 3.49 us -> none  [the longest x1 1.41 us: per_device(): shift = lax.dynamic_slice_in_dim(leaf_shift, subtree, 1, 0)]
    unnamed x13 -> x18, local copies, waits for them, and re-layouts: 4.79 us -> 8.06 us
    pallas_call x1 -> x2, Pallas kernels: 42.3 us -> 45 us  [the longest x1 42.7 us: exchange(): pl.pallas_call(exchange_kernel, out_shape=(jax.ShapeDtypeStruct((4,) + ou...]
where the time goes in v3:
time: 155 us
  Pallas kernels  145 us (94%)
  local copies, waits for them, and re-layouts  8.06 us (5%)
    pallas_call x1, Pallas kernels, exchange(): pl.pallas_call(exchange_kernel, out_shape=(jax.ShapeDtypeStruct((4,) + ou...  42.7 us
    pallas_call x1, Pallas kernels, sum_blocks(): pl.pallas_call(sum_kernel, out_shape=(jax.ShapeDtypeStruct((4, rows, BLK)...  37.3 us
    pallas_call x1, Pallas kernels, per_device(): pl.pallas_call(separator_kernel, out_shape=jax.ShapeDtypeStruct((SSEP //...  36.2 us
    pallas_call x1, Pallas kernels, per_device(): pl.pallas_call(leaf_kernel, out_shape=(jax.ShapeDtypeStruct((KSUP, KSUP /...  26.6 us
    unnamed x18, local copies, waits for them, and re-layouts  8.06 us

profile of v3, /device:TPU:1, one launch (start us, length us, event | category | flops | bytes accessed | tf_op | source)
XLA Modules:
  0.0 155.1 jit_solution(14561583837757084828)
XLA Ops:
  0.6 0.0 copy-start.8
  0.6 2.3 %start_rows.1 = (bf16[64,16,384]{2,1,0:T(8,128)(2,1)}, s32[8,128]{1,0:T(8,128)}, s32[1]{0:T(128)}) custom-call(s32[1]{0:T(128)} %bitcast.1.spot, s32[64]{0:T(128)} %subtree_of.1, bf16[64,16,384]{2,1,0:T(8,128)(2,1)} %bitcast.12, s32[512,128]{1,0:T(8,128)} %bitcast.13), custom_call_target="tpu_custom_call" | custom-call | tf_op jit(solution)/shard_map/start_rows/pallas_call | solution.py:603
  2.9 1.3 pad_add_fusion
  4.2 0.0 copy-start.2
  4.2 1.1 copy-done.2
  5.3 0.0 copy-start.5
  5.3 0.8 copy-done.5
  6.1 0.0 copy-start.6
  6.1 0.7 copy-done.6
  6.8 42.7 %design_exchange.1 = (bf16[4,8,4,2,16,384]{5,4,3,2,1,0:T(8,128)(2,1)S(1)}, f32[1024,12]{1,0:T(8,128)S(1)}) custom-call(bf16[8,4,2,16,384]{4,3,2,1,0:T(8,128)(2,1)S(1)} %bitcast.9, s32[8,128]{1,0:T(8,128)S(1)} %copy-done.6, s32[1]{0:T(128)} %get-tuple-element.13.subtree, s32[12,512]{1,0:T(8,128)S(1)} %bitcast.10), custom_call_target="tpu_custom_call" | custom-call | tf_op jit(solution)/shard_map/design_exchange/pallas_call | solution.py:579
  49.5 0.0 copy-start
  49.5 1.6 %copy-done = bf16[4,8,4,2,16,384]{5,4,3,2,1,0:T(8,128)(2,1)} copy-done((bf16[4,8,4,2,16,384]{5,4,3,2,1,0:T(8,128)(2,1)}, bf16[4,8,4,2,16,384]{5,4,3,2,1,0:T(8,128)(2,1)S(1)}, u32[]{:S(2)}) %copy-start) | copy-done | bytes 3145752
  51.1 0.0 copy-start.4
  51.1 0.8 copy-done.4
  51.9 26.6 %leaf_front.1 = (f32[512,128]{1,0:T(8,128)}, f32[1024,128]{1,0:T(8,128)}, f32[1152,128]{1,0:T(8,128)}) custom-call(s32[2]{0:T(128)} %get-tuple-element.23.spot, bf16[4,1024,384]{2,1,0:T(8,128)(2,1)} %bitcast.8, f32[1024,12]{1,0:T(8,128)} %copy-done.4, f32[64,1536]{1,0:T(8,128)} %shift_rows.1), custom_call_target="tpu_custom_call" | custom-call | tf_op jit(solution)/shard_map/leaf_front/pallas_call | solution.py:625
  78.5 0.0 copy-done.8
  78.5 0.0 copy-start.3
  78.5 1.1 copy-done.3
  79.6 37.3 %separator_sum.1 = (f32[4,1152,128]{2,1,0:T(8,128)S(1)}, f32[4,2,128]{2,1,0:T(2,128)S(1)}) custom-call(f32[1152,128]{1,0:T(8,128)S(1)} %copy-done.3, f32[2,128]{1,0:T(2,128)S(1)} %bitcast.11), custom_call_target="tpu_custom_call" | custom-call | tf_op jit(solution)/shard_map/separator_sum/pallas_call | solution.py:457
  116.9 0.0 copy-start.1
  116.9 1.4 copy-done.1
  118.3 0.0 copy-start.7
  118.3 0.6 copy-done.7
  118.9 36.2 %separator_front.1 = f32[16,256]{1,0:T(8,128)} custom-call(s32[2]{0:T(128)} %get-tuple-element.24.spot, f32[4,1152,128]{2,1,0:T(8,128)} %copy-done.1, f32[4,2,128]{2,1,0:T(2,128)} %copy-done.7), custom_call_target="tpu_custom_call" | custom-call | tf_op jit(solution)/shard_map/separator_front/pallas_call | solution.py:648
Async XLA Ops:
  0.6 77.9 %copy-start.8 = (f32[256]{0:T(256)S(1)}, f32[256]{0:T(256)}, u32[]{:S(2)}) copy-start(f32[256]{0:T(256)} %param.11) | copy-start | bytes 3076
  4.2 1.1 copy-start.2
  5.3 0.8 copy-start.5
  6.1 0.7 copy-start.6
  49.5 1.6 %copy-start = (bf16[4,8,4,2,16,384]{5,4,3,2,1,0:T(8,128)(2,1)}, bf16[4,8,4,2,16,384]{5,4,3,2,1,0:T(8,128)(2,1)S(1)}, u32[]{:S(2)}) copy-start(bf16[4,8,4,2,16,384]{5,4,3,2,1,0:T(8,128)(2,1)S(1)} %get-tuple-element.16) | copy-start | bytes 9437188
  51.1 0.8 copy-start.4
  78.5 1.1 copy-start.3
  116.9 1.4 copy-start.1
  118.3 0.6 copy-start.7

commit v4 on v3

--- a/solution.py
+++ b/solution.py
@@ -11,7 +11,7 @@
 BLK = 128
 SLAB = 16
 HIGHEST = lax.Precision.HIGHEST
-VMEM_LIMIT = 60 << 20
+VMEM_LIMIT = 26 << 20
 
 
 def row_of(values, index):
@@ -138,13 +138,14 @@
 
 
 def leaf_kernel(
-    spot, design, touch, shift_rows, factor_out, coupling_out, blocks_out,
+    subtree_of, design, touch, shift_rows, factor_out, coupling_out, blocks_out,
     masked, front, left, right, trail, inverse_ref, factor_ref, shift,
 ):
-    panel_index = spot[0]
+    panel_index = lax.axis_index("panel")
+    subtree = subtree_of[lax.axis_index("leaf")]
     rows = design.shape[1]
     piece = design.shape[2]
-    shift[...] = shift_rows[pl.ds(spot[1], 1), :]
+    shift[...] = shift_rows[pl.ds(subtree, 1), :]
     for c in range(FRONT // BLK):
         p, at = c * BLK // piece, c * BLK % piece
         keep = jnp.broadcast_to(touch[:, c : c + 1], (rows, BLK)).astype(jnp.bfloat16)
@@ -207,7 +208,7 @@
     lax.fori_loop(0, last + 2, pack, 0)
 
 
-def separator_kernel(spot, blocks, shift, out, matrix, left, right, inverse_ref, factor_ref):
+def separator_kernel(blocks, shift, out, matrix, left, right, inverse_ref, factor_ref):
     size = SSEP // BLK
     share = 1.0 / 64
     row_ids = lax.broadcasted_iota(jnp.int32, (BLK, BLK), 0)
@@ -240,24 +241,9 @@
     lax.fori_loop(0, size - 1, step, 0)
     matrix[: SSEP - BLK, SSEP - BLK :] = jnp.zeros((SSEP - BLK, BLK), jnp.float32)
     matrix[SSEP - BLK :, SSEP - BLK :] = factor_ref[...]
-    top = pl.multiple_of(spot[0] * out.shape[0], out.shape[0])
-    start = pl.multiple_of(spot[1] * out.shape[1], out.shape[1])
+    top = pl.multiple_of(lax.axis_index("leaf") * out.shape[0], out.shape[0])
+    start = pl.multiple_of(lax.axis_index("panel") * out.shape[1], out.shape[1])
     out[...] = matrix[pl.ds(top, out.shape[0]), pl.ds(start, out.shape[1])]
-
-
-def start_kernel(spot, subtree_of, design, cycle_index, outgoing, position, subtree_out):
-    leaves, block_rows, _ = design.shape
-    rows = leaves * block_rows
-    subtree = subtree_of[spot[0]]
-    subtree_out[0] = subtree
-    index = cycle_index[pl.ds(pl.multiple_of(subtree * 8, 8), 8), :]
-    position[...] = (index // rows) * block_rows + index % rows - subtree * block_rows
-
-    def move(d, carry):
-        outgoing[d] = design[subtree_of[d]]
-        return carry
-
-    lax.fori_loop(0, leaves, move, 0, unroll=8)
 
 
 VM = pl.BlockSpec(memory_space=pltpu.VMEM)
@@ -285,15 +271,17 @@
     )
 
 
-def greet(devices):
+def greet(devices, meanwhile=None):
     barrier = pltpu.get_barrier_semaphore()
     for device in devices:
         pl.semaphore_signal(barrier, inc=1, device_id=device, device_id_type=MESH)
+    if meanwhile is not None:
+        meanwhile()
     pl.semaphore_wait(barrier, len(devices))
 
 
-TILES = 18
-STARTS = [15 * i // 7 for i in range(Z)]
+TILES = 9
+CHUNK = 16
 
 
 def sum_kernel(
@@ -304,8 +292,8 @@
 ):
     z, x, y, core = place()
     lo, hi = y % LO, y // LO
-    piece = TILES * 8
-    half = piece // 2
+    half = TILES * 8
+    piece = 2 * half
     plane = [(dx, dy) for dx in range(X) for dy in range(LO) if dx or dy]
 
     def at_plane(dx, dy):
@@ -334,69 +322,81 @@
         pending.append(copy)
         return copy
 
-    def rows_of(x_at, y_at):
-        return pl.multiple_of((x_at * LO + y_at % LO) * piece, 8)
+    def rows_of(x_at, y_at, side=0):
+        return pl.multiple_of((x_at * LO + y_at % LO) * piece + side * half, 8)
 
     def panel_of(y_at, core_at):
         return y_at // LO * 2 + core_at
 
+    first = {}
+    for side in range(2):
+        for dx, dy in plane:
+            i = side * 8 + dx * LO + dy
+            at = rows_of((x + dx) % X, lo + dy, side)
+            first[side, dx, dy] = go(
+                copy_to(
+                    blocks.at[pl.ds(at, half), :], landed_a.at[i], sent_a.at[i], got_a.at[i], at_plane(dx, dy)
+                )
+            )
+
     own_panel = panel_of(y, core)
-    go(copy_to(shift, shifts.at[own_panel], sent_h.at[0], got_h.at[0], at_y(2)))
+    over = go(copy_to(shift, shifts.at[own_panel], sent_h.at[0], got_h.at[0], at_y(2)))
     go(copy_to(shift, shifts.at[own_panel], sent_h.at[1], got_h.at[1], sibling))
-    keep = pltpu.make_async_copy(shift, shifts.at[own_panel], local.at[Z])
+    keep = pltpu.make_async_copy(shift, shifts.at[own_panel], local.at[2 * Z])
     keep.start()
 
-    first = []
-    for dx, dy in plane:
-        i = dx * LO + dy
-        at = rows_of((x + dx) % X, lo + dy)
-        first.append(
-            go(copy_to(blocks.at[pl.ds(at, piece), :], landed_a.at[i], sent_a.at[i], got_a.at[i], at_plane(dx, dy)))
-        )
-    total = blocks[pl.ds(rows_of(x, lo), piece), :]
-    for (dx, dy), copy in zip(plane, first):
-        copy.wait_recv()
-        total = total + landed_a[dx * LO + dy]
-    partial[...] = total
-
     def start_of(z_at):
-        return pl.multiple_of(15 * z_at // 7 * 8, 8)
-
-    second = []
-    for d in range(1, Z):
-        source = partial.at[pl.ds(start_of((z + d) % Z), 24), :]
-        second.append(go(copy_to(source, landed_b.at[d], sent_b.at[d], got_b.at[d], at_z(d))))
-    total = partial[pl.ds(start_of(z), 24), :]
-    for d, copy in zip(range(1, Z), second):
-        copy.wait_recv()
-        total = total + landed_b[d]
-    reduced[...] = total
-
-    third = [
-        go(copy_to(reduced, gathered.at[z], sent_c.at[d], got_c.at[d], at_z(d))) for d in range(1, Z)
-    ]
-    mine = pltpu.make_async_copy(reduced, gathered.at[z], local.at[0])
-    mine.start()
-    pending[0].wait_recv()
-    go(copy_to(shifts.at[panel_of(y + 2 - y // 2 * 4, core)], shifts.at[panel_of(y + 2 - y // 2 * 4, core)],
-               sent_h.at[2], got_h.at[2], sibling))
-    mine.wait()
-    for copy in third:
-        copy.wait_recv()
-    top = rows_of(x, y)
-    own = whole.at[own_panel, pl.ds(top, piece), :]
-    moves = []
-    for i in range(Z):
-        length = ((STARTS + [TILES])[i + 1] - STARTS[i]) * 8
-        move = pltpu.make_async_copy(
-            gathered.at[i, 0:length, :],
-            whole.at[own_panel, pl.ds(pl.multiple_of(top + STARTS[i] * 8, 8), length), :],
-            local.at[i],
-        )
+        return pl.multiple_of(z_at % Z * 8, 8)
+
+    second = {}
+    for side in range(2):
+        total = blocks[pl.ds(rows_of(x, lo, side), half), :]
+        for dx, dy in plane:
+            first[side, dx, dy].wait_recv()
+            total = total + landed_a[side * 8 + dx * LO + dy]
+        partial[side] = total
+        for d in range(1, Z):
+            i = side * Z + d
+            source = partial.at[side, pl.ds(start_of(z + d), CHUNK), :]
+            second[side, d] = go(copy_to(source, landed_b.at[i], sent_b.at[i], got_b.at[i], at_z(d)))
+
+    third, mine = {}, []
+    for side in range(2):
+        total = partial[side, pl.ds(start_of(z), CHUNK), :]
+        for d in range(1, Z):
+            second[side, d].wait_recv()
+            total = total + landed_b[side * Z + d]
+        reduced[side] = total
+        for d in range(1, Z):
+            i = side * Z + d
+            third[side, d] = go(
+                copy_to(reduced.at[side], gathered.at[side, z], sent_c.at[i], got_c.at[i], at_z(d))
+            )
+        move = pltpu.make_async_copy(reduced.at[side], gathered.at[side, z], local.at[side * Z])
         move.start()
-        moves.append(move)
-    for move in moves:
-        move.wait()
+        mine.append(move)
+    over.wait_recv()
+    far = shifts.at[panel_of(y + 2 - y // 2 * 4, core)]
+    go(copy_to(far, far, sent_h.at[2], got_h.at[2], sibling))
+
+    def assemble(side):
+        mine[side].wait()
+        for d in range(1, Z):
+            third[side, d].wait_recv()
+        top = rows_of(x, y, side)
+        moves = []
+        for i in range(Z):
+            length = CHUNK if i == Z - 1 else 8
+            moves.append(
+                pltpu.make_async_copy(
+                    gathered.at[side, i, 0:length, :],
+                    whole.at[own_panel, pl.ds(pl.multiple_of(top + i * 8, 8), length), :],
+                    local.at[side * Z + i],
+                )
+            )
+            moves[-1].start()
+        for move in moves:
+            move.wait()
 
     def part(x_at, y_at, side, core_at=core):
         at = pl.multiple_of(rows_of(x_at, y_at) + side * half, 8)
@@ -408,9 +408,6 @@
     ring = [at_y, at_x]
     length = Y
     first_wave = {}
-    for side in range(2):
-        for d in range(1, length):
-            first_wave[side, d] = pass_on(part(x, y, side), sent_1, got_1, side * 4 + d, ring[side](d))
     second_wave = []
 
     def spread(side, d):
@@ -422,6 +419,9 @@
         pass_on(where, sent_s, got_s, (side * 4 + d) * 4, sibling)
 
     for side in range(2):
+        assemble(side)
+        for d in range(1, length):
+            first_wave[side, d] = pass_on(part(x, y, side), sent_1, got_1, side * 4 + d, ring[side](d))
         spread(side, 0)
     for d in range(1, length):
         for side in range(2):
@@ -463,15 +463,15 @@
         in_specs=[VM, VM],
         out_specs=(VM, VM),
         scratch_shapes=[
-            pltpu.VMEM((8, TILES * 8, BLK), f32),
-            pltpu.VMEM((TILES * 8, BLK), f32),
-            pltpu.VMEM((Z, 24, BLK), f32),
-            pltpu.VMEM((24, BLK), f32),
-            pltpu.VMEM((Z, 24, BLK), f32),
-            dma((8,)), dma((8,)), dma((8,)), dma((8,)), dma((8,)), dma((8,)), dma((Z + 1,)),
+            pltpu.VMEM((16, TILES * 8, BLK), f32),
+            pltpu.VMEM((2, TILES * 8, BLK), f32),
+            pltpu.VMEM((2 * Z, CHUNK, BLK), f32),
+            pltpu.VMEM((2, CHUNK, BLK), f32),
+            pltpu.VMEM((2, Z, CHUNK, BLK), f32),
+            dma((16,)), dma((16,)), dma((16,)), dma((16,)), dma((16,)), dma((16,)), dma((2 * Z + 1,)),
             dma((8,)), dma((8,)), dma((32,)), dma((32,)), dma((32,)), dma((32,)), dma((3,)), dma((3,)),
         ],
-        compiler_params=pltpu.CompilerParams(collective_id=1, has_side_effects=True, vmem_limit_bytes=40 << 20),
+        compiler_params=pltpu.CompilerParams(collective_id=1, has_side_effects=True, vmem_limit_bytes=16 << 20),
         name="separator_sum",
     )(blocks, shift)
 
@@ -502,8 +502,8 @@
 
 
 def exchange_kernel(
-    outgoing, position, subtree, fill, design, touch,
-    middle, local, sent_a, got_a, sent_y, got_y, sent_s, got_s,
+    subtree_of, start, cycle_index, fill, design, touch,
+    outgoing, middle, local, sent_a, got_a, sent_y, got_y, sent_s, got_s,
 ):
     z, x, y, core = place()
     own_panel = y // LO * 2 + core
@@ -516,7 +516,11 @@
     def at_y(d):
         return device_at(z, x, (y + d) % Y, core)
 
-    greet([at(*d) for d in near] + [at_y(d) for d in range(1, Y)] + [sibling])
+    def order_blocks():
+        for d in range(Z * X * LO):
+            outgoing[d // (X * LO), d // LO % X, d % LO] = start[subtree_of[d]]
+
+    greet([at(*d) for d in near] + [at_y(d) for d in range(1, Y)] + [sibling], order_blocks)
     pending = []
 
     def go(copy):
@@ -534,7 +538,12 @@
                 outgoing.at[(z + dz) % Z, (x + dx) % X], middle.at[z, x], sent_a.at[i], got_a.at[i], at(dz, dx)
             )
         )
-    touch[...] = row_pattern(subtree[0], position[...], fill)
+    block_rows = start.shape[1]
+    rows = start.shape[0] * block_rows
+    subtree = subtree_of[lax.axis_index("leaf")]
+    index = cycle_index[subtree]
+    position = (index // rows) * block_rows + index % rows - subtree * block_rows
+    touch[...] = row_pattern(subtree, position, fill)
     along = {}
     moves = []
 
@@ -573,22 +582,28 @@
             copy_to(slab(dz, d), slab(dz, d), sent_s.at[i], got_s.at[i], sibling).wait_recv()
 
 
-def exchange(outgoing, position, subtree, fill):
+def exchange(subtree_of, start, cycle_index, fill):
     dma = pltpu.SemaphoreType.DMA
-    rows, piece = outgoing.shape[-2:]
+    shape = (Z, X, LO) + start.shape[1:]
     return pl.pallas_call(
         exchange_kernel,
         out_shape=(
-            jax.ShapeDtypeStruct((4,) + outgoing.shape, outgoing.dtype),
-            jax.ShapeDtypeStruct((position.size, fill.shape[0]), jnp.float32),
+            jax.ShapeDtypeStruct((4,) + shape, start.dtype),
+            jax.ShapeDtypeStruct((cycle_index.size // start.shape[0], fill.shape[0]), jnp.float32),
         ),
-        in_specs=[VM, VM, SM, VM],
+        in_specs=[SM, VM, VM, VM],
         out_specs=(VM, VM),
-        scratch_shapes=[pltpu.VMEM(outgoing.shape, outgoing.dtype), dma((Z + 1,))]
+        scratch_shapes=[
+            pltpu.VMEM(shape, start.dtype),
+            pltpu.VMEM(shape, start.dtype),
+            dma((Z + 1,)),
+        ]
         + [dma((Z * X,)) for _ in range(6)],
-        compiler_params=pltpu.CompilerParams(collective_id=2, has_side_effects=True, vmem_limit_bytes=40 << 20),
+        compiler_params=pltpu.CompilerParams(
+            collective_id=2, has_side_effects=True, vmem_limit_bytes=20 << 20
+        ),
         name="design_exchange",
-    )(outgoing, position, subtree, fill)
+    )(subtree_of, start, cycle_index, fill)
 
 
 def per_device(
@@ -598,27 +613,11 @@
     panels = lax.axis_size("panel")
     rows, piece = pix_cycle.shape
     block_rows = rows // leaves
-    leaf_index = lax.axis_index("leaf")
-    panel_index = lax.axis_index("panel")
-    outgoing, position, subtree = pl.pallas_call(
-        start_kernel,
-        out_shape=(
-            jax.ShapeDtypeStruct((leaves, block_rows, piece), pix_cycle.dtype),
-            jax.ShapeDtypeStruct((8, BLK), jnp.int32),
-            jax.ShapeDtypeStruct((1,), jnp.int32),
-        ),
-        in_specs=[SM, SM, VM, VM],
-        out_specs=(VM, VM, SM),
-        compiler_params=pltpu.CompilerParams(vmem_limit_bytes=VMEM_LIMIT),
-        name="start_rows",
-    )(
-        leaf_index[None],
+    received, touch = exchange(
         subtree_of,
         pix_cycle.reshape(leaves, block_rows, piece),
-        cycle_to_dissection.reshape(-1, BLK),
-    )
-    received, touch = exchange(
-        outgoing.reshape(Z, X, LO, block_rows, piece), position, subtree, fill_blocks.T
+        cycle_to_dissection.reshape(leaves, rows // BLK, BLK),
+        fill_blocks.T,
     )
     design = received.reshape(panels, rows, piece)
     count = SSEP // BLK + 1
@@ -643,12 +642,12 @@
         ],
         compiler_params=pltpu.CompilerParams(vmem_limit_bytes=VMEM_LIMIT),
         name="leaf_front",
-    )(jnp.stack([panel_index, subtree[0]]), design, touch, leaf_shift)
+    )(subtree_of, design, touch, leaf_shift)
     whole, shifts = sum_blocks(blocks, separator_shift.reshape(2, BLK))
     result_rows = pl.pallas_call(
         separator_kernel,
         out_shape=jax.ShapeDtypeStruct((SSEP // leaves, SSEP // panels), jnp.float32),
-        in_specs=[SM, VM, VM],
+        in_specs=[VM, VM],
         out_specs=VM,
         scratch_shapes=[
             pltpu.VMEM((SSEP, SSEP), jnp.float32),
@@ -659,7 +658,7 @@
         ],
         compiler_params=pltpu.CompilerParams(vmem_limit_bytes=VMEM_LIMIT),
         name="separator_front",
-    )(jnp.stack([leaf_index, panel_index]), whole, shifts)
+    )(whole, shifts)
     return (factor_cols, coupling_cols, result_rows)
 
 

time: 155 us -> 145 us (0.935)
  Pallas kernels: 145 us -> 139 us
  local copies, waits for them, and re-layouts: 8.06 us -> 5.14 us
    unnamed x18 -> x14, local copies, waits for them, and re-layouts: 8.06 us -> 5.14 us
    pallas_call x2 -> x1, Pallas kernels: 45 us -> 42.4 us  [exchange(): pl.pallas_call(exchange_kernel, out_shape=(jax.ShapeDtypeStruct((4,) + sh...]
    pallas_call x1, Pallas kernels: 26.6 us -> 24.9 us  [per_device(): pl.pallas_call(leaf_kernel, out_shape=(jax.ShapeDtypeStruct((KSUP, KSUP /...]
    pallas_call x1, Pallas kernels: 36.2 us -> 34.5 us  [per_device(): pl.pallas_call(separator_kernel, out_shape=jax.ShapeDtypeStruct((SSEP //...]
where the time goes in v4:
time: 145 us
  Pallas kernels  139 us (96%)
  local copies, waits for them, and re-layouts  5.14 us (4%)
    pallas_call x1, Pallas kernels, exchange(): pl.pallas_call(exchange_kernel, out_shape=(jax.ShapeDtypeStruct((4,) + sh...  42.4 us
    pallas_call x1, Pallas kernels, sum_blocks(): pl.pallas_call(sum_kernel, out_shape=(jax.ShapeDtypeStruct((4, rows, BLK)...  37.1 us
    pallas_call x1, Pallas kernels, per_device(): pl.pallas_call(separator_kernel, out_shape=jax.ShapeDtypeStruct((SSEP //...  34.5 us
    pallas_call x1, Pallas kernels, per_device(): pl.pallas_call(leaf_kernel, out_shape=(jax.ShapeDtypeStruct((KSUP, KSUP /...  24.9 us
    unnamed x14, local copies, waits for them, and re-layouts  5.14 us

profile of v4, /device:TPU:1, one launch (start us, length us, event | category | flops | bytes accessed | tf_op | source)
XLA Modules:
  0.0 144.7 jit_solution(4227715243871821252)
XLA Ops:
  0.6 0.0 copy-start.6
  0.6 0.0 copy-start
  0.7 1.1 copy-done
  1.8 0.0 copy-start.2
  1.8 0.9 copy-done.2
  2.7 0.0 copy-start.3
  2.7 0.8 copy-done.3
  3.5 0.0 copy-start.4
  3.5 0.7 copy-done.4
  4.1 42.4 %design_exchange.1 = (bf16[4,8,4,2,16,384]{5,4,3,2,1,0:T(8,128)(2,1)S(1)}, f32[1024,12]{1,0:T(8,128)S(1)}) custom-call(s32[64]{0:T(128)S(1)} %copy-done.4, bf16[64,16,384]{2,1,0:T(8,128)(2,1)S(1)} %bitcast.6, s32[64,8,128]{2,1,0:T(8,128)S(1)} %bitcast.7, s32[12,512]{1,0:T(8,128)S(1)} %bitcast.8), custom_call_target="tpu_custom_call" | custom-call | tf_op jit(solution)/shard_map/design_exchange/pallas_call | solution.py:588
  46.6 0.0 copy-start.1
  46.6 1.0 copy-done.1
  47.6 0.0 copy-start.5
  47.6 0.7 copy-done.5
  48.2 24.9 %leaf_front.1 = (f32[512,128]{1,0:T(8,128)}, f32[1024,128]{1,0:T(8,128)}, f32[1152,128]{1,0:T(8,128)S(1)}) custom-call(s32[64]{0:T(128)S(1)} %copy-done.5, bf16[4,1024,384]{2,1,0:T(8,128)(2,1)S(1)} %bitcast.5, f32[1024,12]{1,0:T(8,128)S(1)} %get-tuple-element.11.touch, f32[64,1536]{1,0:T(8,128)S(1)} %copy-done.1), custom_call_target="tpu_custom_call" | custom-call | tf_op jit(solution)/shard_map/leaf_front/pallas_call | solution.py:624
  73.1 0.0 copy-done.6
  73.1 37.1 %separator_sum.1 = (f32[4,1152,128]{2,1,0:T(8,128)S(1)}, f32[4,2,128]{2,1,0:T(2,128)S(1)}) custom-call(f32[1152,128]{1,0:T(8,128)S(1)} %get-tuple-element.14.blocks, f32[2,128]{1,0:T(2,128)S(1)} %bitcast.9), custom_call_target="tpu_custom_call" | custom-call | tf_op jit(solution)/shard_map/separator_sum/pallas_call | solution.py:457
  110.1 34.5 %separator_front.1 = f32[16,256]{1,0:T(8,128)} custom-call(f32[4,1152,128]{2,1,0:T(8,128)S(1)} %get-tuple-element.15.blocks, f32[4,2,128]{2,1,0:T(2,128)S(1)} %get-tuple-element.16.shift), custom_call_target="tpu_custom_call" | custom-call | tf_op jit(solution)/shard_map/separator_front/pallas_call | solution.py:647
Async XLA Ops:
  0.6 72.4 %copy-start.6 = (f32[256]{0:T(256)S(1)}, f32[256]{0:T(256)}, u32[]{:S(2)}) copy-start(f32[256]{0:T(256)} %param.11) | copy-start | bytes 3076
  0.6 1.1 copy-start
  1.8 0.9 copy-start.2
  2.7 0.8 copy-start.3
  3.5 0.7 copy-start.4
  46.6 1.0 copy-start.1
  47.6 0.7 copy-start.5
